TPU v7x, 128 devices: a whole 4x4x4 slice. The times are simulated.
128 devices in a mesh: subj: 32 (over z, y, core), vox: 4 (over x).
Axes of the slice: x: 4, y: 4, z: 4, core: 2. Of those that a mesh axis runs over, the one named last changes fastest.
Arguments:
- scans: bfloat16 [20480, 49152], P('subj', 'vox'), may hold values from -6 to 6
- test_matrix: bfloat16 [49152, 128], P('vox'), may hold values from -6 to 6
- lengths: int32 [32], replicated, may hold values from 160 to 640, as said below
- block_subject: int32 [32], replicated, may hold values from 0 to 31, each once
Outputs:
- basis: float32 [49152, 128], P('vox')
Inputs may be any that keep to these rules, and one draw needn't show every extreme that they name: `lengths`: one subject has exactly 640 rows and one exactly 160. `block_subject`: each subject appears once.
All inputs are finite; a program needn't handle non-finite values.
Results may differ from a plain program's by a relative error of at most 0.0046.
Values may be sent and summed in bfloat16 or wider, within the bound.
A program may use at most 128 MiB of HBM per device.

v0:
```python
import jax
import jax.numpy as jnp
from jax import lax
from jax.sharding import PartitionSpec as P

V = 49152
PASSES = 2


def on_device(scans, test_matrix, lengths, block_subject):
    time_rows, voxel_cols = scans.shape
    rank_cols = test_matrix.shape[1]
    position = lax.axis_index("subj")
    slot_ids = jnp.arange(block_subject.shape[0], dtype=jnp.int32)
    subject = jnp.sum(jnp.where(slot_ids == position, block_subject, 0))
    length = jnp.sum(jnp.where(slot_ids == subject, lengths, 0))
    live_rows = (jnp.arange(time_rows, dtype=jnp.int32) < length)[:, None]
    panel_now = test_matrix
    result = jnp.zeros((voxel_cols, rank_cols), jnp.float32)
    for sweep_index in range(PASSES):
        partial_scores = jnp.dot(scans, panel_now, preferred_element_type=jnp.float32)
        summed = lax.psum(partial_scores, "vox")
        scores = jnp.where(live_rows, summed, jnp.float32(0.0)).astype(jnp.bfloat16)
        sketch = lax.psum(
            lax.dot_general(
                scans, scores, (((0,), (0,)), ((), ())), preferred_element_type=jnp.float32
            ),
            "subj",
        )
        local_gram = jnp.dot(sketch.T, sketch, precision=lax.Precision.HIGHEST)
        gram_matrix = lax.psum(local_gram, "vox") / V
        factor = jnp.linalg.cholesky(gram_matrix)
        orthonormal = jax.scipy.linalg.solve_triangular(factor, sketch.T, lower=True).T
        panel_now = orthonormal.astype(jnp.bfloat16)
        result = orthonormal
    return result


def solution(mesh):
    placed = (P("subj", "vox"), P("vox", None), P(), P())
    return jax.shard_map(
        on_device, mesh=mesh, in_specs=placed, out_specs=P("vox", None), check_vma=False
    )
```

profile of v0, /device:TPU:1, one launch (start us, length us, event | category | flops | bytes accessed | tf_op | source)
XLA Modules:
  0.0 499.3 jit_solution(9757382926580311608)
XLA Ops:
  6.5 1.4 fusion.14
  8.0 2.0 fusion.15
  10.7 8.4 %fusion.18 = f32[640,128]{1,0:T(8,128)} fusion(bf16[640,12288]{1,0:T(8,128)(2,1)} %param.7, bf16[12288,128]{1,0:T(8,128)(2,1)S(1)} %copy-done), kind=kOutput, calls=%fused_computation.39 | convolution fusion | flops 2013265920 | bytes 19202048 | tf_op jit(solution)/shard_map/dot_general | solution.py:21
  19.1 17.7 %all-reduce.14 = bf16[640,128]{1,0:T(8,128)(2,1)S(1)} all-reduce(f32[640,128]{1,0:T(8,128)} %fusion.18), channel_id=1, replica_groups=mesh['subj'=32,'vox'=4] {'vox'}, use_global_device_ids=true, to_apply=%region_2.3 | all-reduce | flops 81920 | bytes 491520 | tf_op jit(solution)/shard_map/psum | solution.py:22
  36.8 11.0 %convolution_bitcast_fusion.1 = f32[12288,128]{0,1:T(8,128)} fusion(bf16[640,12288]{1,0:T(8,128)(2,1)} %param.7, bf16[640,128]{1,0:T(8,128)(2,1)S(1)} %all-reduce.14, pred[640]{0:T(1024)(128)(4,1)S(1)} %iota_compare_fusion.2), kind=kOutput, calls=%fused_computation.1 | convolution fusion | flops 2013347840 | bytes 22184576 | tf_op jit(solution)/shard_map/dot_general | solution.py:25
  47.8 120.9 %all-reduce.7.cloned.1.call-done = f32[12288,128]{0,1:T(8,128)} async-done(((f32[12288,128]{0,1:T(8,128)}), f32[12288,128]{0,1:T(8,128)}) %all-reduce.7.cloned.1.call-update) | async-done | bytes 6291472 | tf_op jit(solution)/shard_map/psum | solution.py:24
  168.7 8.8 %fusion.19 = f32[128,128]{0,1:T(8,128)} fusion(f32[12288,128]{0,1:T(8,128)} %all-reduce.7.cloned.1.call-done), kind=kOutput, calls=%fused_computation.40 | convolution fusion | flops 2415919104 | bytes 6356992 | tf_op jit(solution)/shard_map/dot_general | solution.py:30
  177.8 38.6 %all-reduce.9.cloned.1.call-done = f32[128,128]{0,1:T(8,128)} async-done(((f32[128,128]{0,1:T(8,128)}), f32[128,128]{0,1:T(8,128)}) %all-reduce.9.cloned.1.call-update) | async-done | bytes 65552 | tf_op jit(solution)/shard_map/psum | solution.py:31
  216.4 0.8 broadcast_multiply_fusion.1
  217.3 0.9 fusion.11
  218.2 11.7 %cholesky.44 = f32[128,128]{1,0:T(8,128)S(1)} custom-call(f32[128,128]{1,0:T(8,128)S(1)} %fusion.11), custom_call_target="Cholesky" | custom-call | tf_op jit(solution)/shard_map/jit(cholesky)/cholesky | solution.py:32
  231.2 9.8 %custom-call.6 = f32[1,128,128]{1,2,0:T(8,128)S(1)} custom-call(f32[1,128,128]{2,1,0:T(8,128)S(1)} %fusion.6), custom_call_target="InvertDiagBlocksLowerTriangular" | custom-call | tf_op jit(solution)/shard_map/jit(_solve_triangular)/triangular_solve | solution.py:33
  241.0 7.6 %convolution_convert_fusion = bf16[128,12288]{1,0:T(8,128)(2,1)S(1)} fusion(f32[12288,128]{0,1:T(8,128)} %all-reduce.7.cloned.1.call-done, f32[1,128,128]{1,2,0:T(8,128)S(1)} %custom-call.6), kind=kOutput, calls=%fused_computation.3 | convolution fusion | flops 2417491968 | bytes 9502720 | tf_op jit(solution)/shard_map/jit(_solve_triangular)/triangular_solve | solution.py:33
  248.6 7.7 %convolution_bitcast_fusion.3 = f32[640,128]{1,0:T(8,128)S(1)} fusion(bf16[128,12288]{1,0:T(8,128)(2,1)S(1)} %convolution_convert_fusion, bf16[640,12288]{1,0:T(8,128)(2,1)} %param.7), kind=kOutput, calls=%fused_computation.6 | convolution fusion | flops 2013265920 | bytes 19202048 | tf_op jit(solution)/shard_map/dot_general | solution.py:21
  256.3 17.5 %all-reduce.15 = bf16[640,128]{1,0:T(8,128)(2,1)} all-reduce(f32[640,128]{1,0:T(8,128)S(1)} %convolution_bitcast_fusion.3), channel_id=1, replica_groups=mesh['subj'=32,'vox'=4] {'vox'}, use_global_device_ids=true, to_apply=%region_7.10 | all-reduce | flops 81920 | bytes 491520 | tf_op jit(solution)/shard_map/psum | solution.py:22
  273.8 11.1 %convolution_bitcast_fusion = f32[12288,128]{0,1:T(8,128)} fusion(bf16[640,12288]{1,0:T(8,128)(2,1)} %param.7, bf16[640,128]{1,0:T(8,128)(2,1)} %all-reduce.15, pred[640]{0:T(1024)(128)(4,1)S(1)} %iota_compare_fusion.2), kind=kOutput, calls=%fused_computation | convolution fusion | flops 2013347840 | bytes 22184576 | tf_op jit(solution)/shard_map/dot_general | solution.py:25
  285.2 119.5 %all-reduce.11.cloned.1.call-done = f32[12288,128]{0,1:T(8,128)} async-done(((f32[12288,128]{0,1:T(8,128)}), f32[12288,128]{0,1:T(8,128)}) %all-reduce.11.cloned.1.call-update) | async-done | bytes 6291472 | tf_op jit(solution)/shard_map/psum | solution.py:24
  404.7 8.8 %fusion.20 = f32[128,128]{0,1:T(8,128)} fusion(f32[12288,128]{0,1:T(8,128)} %all-reduce.11.cloned.1.call-done), kind=kOutput, calls=%fused_computation.41 | convolution fusion | flops 2415919104 | bytes 6356992 | tf_op jit(solution)/shard_map/dot_general | solution.py:30
  413.5 38.8 %all-reduce.13.cloned.1.call-done = f32[128,128]{0,1:T(8,128)} async-done(((f32[128,128]{0,1:T(8,128)}), f32[128,128]{0,1:T(8,128)}) %all-reduce.13.cloned.1.call-update) | async-done | bytes 65552 | tf_op jit(solution)/shard_map/psum | solution.py:31
  453.3 0.9 fusion.9
  454.2 11.7 %cholesky.55 = f32[128,128]{1,0:T(8,128)S(1)} custom-call(f32[128,128]{1,0:T(8,128)S(1)} %fusion.9), custom_call_target="Cholesky" | custom-call | tf_op jit(solution)/shard_map/jit(cholesky)/cholesky | solution.py:32
  467.2 9.8 %custom-call.7 = f32[1,128,128]{1,2,0:T(8,128)S(1)} custom-call(f32[1,128,128]{2,1,0:T(8,128)S(1)} %fusion.7), custom_call_target="InvertDiagBlocksLowerTriangular" | custom-call | tf_op jit(solution)/shard_map/jit(_solve_triangular)/triangular_solve | solution.py:33
  477.0 9.2 %convolution_bitcast_fusion.2 = f32[12288,128]{0,1:T(8,128)} fusion(f32[12288,128]{0,1:T(8,128)} %all-reduce.11.cloned.1.call-done, f32[1,128,128]{1,2,0:T(8,128)S(1)} %custom-call.7), kind=kOutput, calls=%fused_computation.2 | convolution fusion | flops 2415919104 | bytes 12648448 | tf_op jit(solution)/shard_map/jit(_solve_triangular)/triangular_solve | solution.py:33
  486.3 6.6 %copy.9 = f32[12288,128]{1,0:T(8,128)} copy(f32[12288,128]{0,1:T(8,128)} %convolution_bitcast_fusion.2) | data formatting | bytes 12582912 | tf_op jit(solution)/shard_map/transpose | solution.py:33
  (20 shorter events, 5.0 us)
Async XLA Ops:
  6.5 4.2 copy-start
  6.5 162.2 %all-reduce.7.cloned.1.call-start = ((), (), s32[]{:S(2)}) async-start(), calls=%async_computation | async-start | bytes 12582912 | tf_op jit(solution)/shard_map/psum | solution.py:24
  47.8 168.6 %all-reduce.9.cloned.1.call-start = ((), (), s32[]{:S(2)}) async-start(), calls=%async_computation.1 | async-start | bytes 131072 | tf_op jit(solution)/shard_map/psum | solution.py:31
  177.6 227.1 %all-reduce.11.cloned.1.call-start = ((), (), s32[]{:S(2)}) async-start(), calls=%async_computation.2 | async-start | bytes 12582912 | tf_op jit(solution)/shard_map/psum | solution.py:24
  284.9 167.5 %all-reduce.13.cloned.1.call-start = ((), (), s32[]{:S(2)}) async-start(), calls=%async_computation.3 | async-start | bytes 131072 | tf_op jit(solution)/shard_map/psum | solution.py:31
Sparse Core Ops, SparseCore 0:
  47.9 120.7 all-reduce.6
  177.7 38.6 all-reduce.8
  285.0 119.6 all-reduce.10
  413.7 38.6 all-reduce.12
where the time goes:
time: 501 us; the launch traced here: 499 us
  waiting for transfers between devices  318 us (63%)
  matrix products  72.6 us (14%)
  other arithmetic  53.3 us (11%)
  blocking collectives  35.2 us (7%)
  between operations  13.2 us (3%)
  local copies, waits for them, and re-layouts  6.73 us (1%)
    psum x2, waiting for transfers between devices, on_device(): lax.psum(lax.dot_general(scans, scores, (((0,), (0,)), ((), ())), preferr...  240 us
    psum x2, waiting for transfers between devices, on_device(): gram_matrix = lax.psum(local_gram, 'vox') / V  77.4 us
    psum x2, blocking collectives, on_device(): summed = lax.psum(partial_scores, 'vox')  35.2 us
    another operation x6, other arithmetic, on_device(): factor = jnp.linalg.cholesky(gram_matrix)  24.8 us
    dot_general x2, matrix products, on_device(): lax.dot_general(scans, scores, (((0,), (0,)), ((), ())), preferred_elemen...  22 us
    another operation x4, other arithmetic, on_device(): jax.scipy.linalg.solve_triangular(factor, sketch.T, lower=True)  20.9 us
    dot_general x2, matrix products, on_device(): local_gram = jnp.dot(sketch.T, sketch, precision=lax.Precision.HIGHEST)  17.6 us
    another operation x2, matrix products, on_device(): jax.scipy.linalg.solve_triangular(factor, sketch.T, lower=True)  16.8 us
  transfers between devices with their start and end apart: 4, of which 4 were waited for; matrix products, arithmetic and copies ran while one was open for 0% of the time, Pallas kernels for 0%

commit v1 on v0

v1 whole, which is shorter than its diff:
```python
import functools

import jax
import jax.numpy as jnp
from jax import lax
from jax.experimental import pallas as pl
from jax.experimental.pallas import tpu as pltpu
from jax.sharding import PartitionSpec as P

V = 49152
PASSES = 2
MESH = pl.DeviceIdType.MESH
VMEM_BYTES = 60 * 2**20
ANY = pl.BlockSpec(memory_space=pl.ANY)
VMEM = pl.BlockSpec(memory_space=pltpu.VMEM)
SMEM = pl.BlockSpec(memory_space=pltpu.SMEM)
ORDERS = (("ya", "yb", "za", "zb"), ("yb", "ya", "zb", "za"), ("za", "zb", "ya", "yb"), ("zb", "za", "yb", "ya"))


def ring_bits(i):
    b = lax.div(i, 2)
    return lax.rem(i + b, 2), b


def flip_a(i):
    return i + 1 - 2 * lax.rem(i, 2)


def flip_b(i):
    return 3 - i


class Place:
    def __init__(self):
        here = lax.axis_index("subj")
        self.z, self.y, self.c = lax.div(here, 8), lax.rem(lax.div(here, 2), 4), lax.rem(here, 2)
        self.x = lax.axis_index("vox")
        self.bits = place_bits(self.z, self.y)

    def sibling(self):
        return {"subj": self.z * 8 + self.y * 2 + 1 - self.c}

    def across(self, bit):
        z, y = self.z, self.y
        if bit[0] == "x":
            return {"vox": flip_a(self.x) if bit == "xa" else flip_b(self.x)}
        if bit[0] == "y":
            y = flip_a(y) if bit == "ya" else flip_b(y)
        else:
            z = flip_a(z) if bit == "za" else flip_b(z)
        return {"subj": z * 8 + y * 2 + self.c}


def place_bits(z, y):
    ya, yb = ring_bits(y)
    za, zb = ring_bits(z)
    return {"ya": ya, "yb": yb, "za": za, "zb": zb}


def index_in(order, bits):
    return 8 * bits[order[0]] + 4 * bits[order[1]] + 2 * bits[order[2]] + bits[order[3]]


def meet(devices):
    barrier = pltpu.get_barrier_semaphore()
    for device in devices:
        pl.semaphore_signal(barrier, inc=1, device_id=device, device_id_type=MESH)
    pl.semaphore_wait(barrier, len(devices))


def send(src, dst, send_sem, recv_sem, device):
    copy = pltpu.make_async_remote_copy(
        src_ref=src, dst_ref=dst, send_sem=send_sem, recv_sem=recv_sem, device_id=device, device_id_type=MESH
    )
    copy.start()
    return copy


def scores_kernel(lengths, block_subject, scans, panel, out, held, part, got, full, load_sem, s1, r1, s2, r2):
    x = lax.axis_index("vox")
    rows = part.shape[1]
    depth = panel.shape[0]
    owners = [lax.rem(x + step, 4) for step in (2, 1, 3, 0)]
    loads = []
    for t in range(4):
        start = pl.multiple_of(owners[t] * rows, rows)
        loads.append(pltpu.make_async_copy(scans.at[pl.ds(start, rows)], held.at[t], load_sem.at[t]))
        loads[t].start()
    meet([{"vox": owners[t]} for t in range(3)])
    tile = 3072
    copies = []
    for t in range(4):
        loads[t].wait()

        def add(k, acc, t=t):
            at = pl.multiple_of(k * tile, tile)
            return acc + jnp.dot(
                held[t, :, pl.ds(at, tile)], panel[pl.ds(at, tile), :], preferred_element_type=jnp.float32
            )

        part[t] = lax.fori_loop(0, depth // tile, add, jnp.zeros(part.shape[1:], jnp.float32))
        if t < 3:
            copies.append(send(part.at[t], got.at[t], s1.at[t], r1.at[t], {"vox": owners[t]}))
    total = part[3]
    for t in range(3):
        copies[t].wait()
        total = total + got[t]
    length = lengths[block_subject[lax.axis_index("subj")]]
    time_ids = x * rows + lax.broadcasted_iota(jnp.int32, total.shape, 0)
    full[x] = jnp.where(time_ids < length, total, jnp.float32(0.0)).astype(jnp.bfloat16)
    copies = [send(full.at[x], full.at[x], s2.at[t], r2.at[t], {"vox": owners[t]}) for t in range(3)]
    for copy in copies:
        copy.wait()
    for i in range(4):
        out[pl.ds(i * rows, rows), :] = full[i]


def scores_call(lengths, block_subject, scans, panel, number):
    time_rows, cols = scans.shape
    rank = panel.shape[1]
    rows = time_rows // 4
    return pl.pallas_call(
        scores_kernel,
        out_shape=jax.ShapeDtypeStruct((time_rows, rank), jnp.bfloat16),
        in_specs=[SMEM, SMEM, ANY, VMEM],
        out_specs=VMEM,
        scratch_shapes=[
            pltpu.VMEM((4, rows, cols), jnp.bfloat16),
            pltpu.VMEM((4, rows, rank), jnp.float32),
            pltpu.VMEM((3, rows, rank), jnp.float32),
            pltpu.VMEM((4, rows, rank), jnp.bfloat16),
            pltpu.SemaphoreType.DMA((4,)),
            pltpu.SemaphoreType.DMA((3,)),
            pltpu.SemaphoreType.DMA((3,)),
            pltpu.SemaphoreType.DMA((3,)),
            pltpu.SemaphoreType.DMA((3,)),
        ],
        compiler_params=pltpu.CompilerParams(
            collective_id=number, has_side_effects=True, vmem_limit_bytes=VMEM_BYTES
        ),
        name=f"scores_{number}",
    )(lengths, block_subject, scans, panel)


def sketch_kernel(
    scans, scores, z_out, g_out, held, away, arrived, mine, in1, in2, in3, in4, g_part, g_in, g_sum, g_last,
    load_sem, sc, rc, ss, rs, sg, rg,
):
    place = Place()
    width = held.shape[2]
    rank, piece = z_out.shape
    quarter = rank // 4
    slots = held.shape[0]

    def block_of(t):
        core = lax.rem(place.c + 1 + t // 4, 2)
        return core * 16 + (t % 4) * 4

    def load(t):
        start = pl.multiple_of(block_of(t) * piece, width)
        return pltpu.make_async_copy(scans.at[:, pl.ds(start, width)], held.at[t % slots], load_sem.at[t % slots])

    for t in range(slots - 1):
        load(t).start()
    bits7 = ("xa", "xb", "ya", "yb", "za", "zb")
    meet([place.sibling()] + [place.across(bit) for bit in bits7])
    left = scores[...].T
    core_copies = []
    for t in range(8):
        if t + slots - 1 < 8:
            load(t + slots - 1).start()
        load(t).wait()
        z = t % 4
        block = jnp.dot(left, held[t % slots], preferred_element_type=jnp.float32)
        if t >= 4:
            core_copies[z].wait()
        for y in range(4):
            bits = place_bits(jnp.int32(z), jnp.int32(y))
            for q in range(4):
                value = block[q * quarter : (q + 1) * quarter, y * piece : (y + 1) * piece]
                if t < 4:
                    away[z, q, y] = value
                else:
                    mine[q, static_index(ORDERS[q], z, y)] = value + arrived[z, q, y]
        if t < 4:
            core_copies.append(send(away.at[z], arrived.at[z], sc.at[z], rc.at[z], place.sibling()))

    offset = [jnp.int32(0)] * 4
    for stage, inbox in enumerate((in1, in2, in3, in4)):
        half = 8 >> stage
        copies = []
        for q in range(4):
            bit = ORDERS[q][stage]
            there = offset[q] + (1 - place.bits[bit]) * half
            n = stage * 4 + q
            copies.append(
                send(mine.at[q, pl.ds(there, half)], inbox.at[q], ss.at[n], rs.at[n], place.across(bit))
            )
            offset[q] = offset[q] + place.bits[bit] * half
        for q in range(4):
            copies[q].wait()

            def add(i, carry, q=q, inbox=inbox):
                at = offset[q] + i
                mine[q, at] = mine[q, at] + inbox[q, i]
                return carry

            lax.fori_loop(0, half, add, 0)
    for q in range(4):
        z_out[pl.ds(q * quarter, quarter), :] = mine[q, offset[q]]

    own = z_out[...]
    gram = lax.dot_general(
        own, own, (((1,), (1,)), ((), ())), precision=lax.Precision.HIGHEST, preferred_element_type=jnp.float32
    )
    rows = rank // 2
    g_part[0] = gram[:rows]
    g_part[1] = gram[rows:]
    copy = send(g_part.at[1 - place.c], g_in.at[0], sg.at[0], rg.at[0], place.sibling())
    copy.wait()
    g_sum[0] = g_part[place.c] + g_in[0]
    for n, bit in enumerate(bits7):
        copy = send(g_sum.at[n], g_in.at[n + 1], sg.at[n + 1], rg.at[n + 1], place.across(bit))
        copy.wait()
        g_sum[n + 1] = g_sum[n] + g_in[n + 1]
    g_last[place.c] = g_sum[6]
    copy = send(g_last.at[place.c], g_last.at[place.c], sg.at[7], rg.at[7], place.sibling())
    copy.wait()
    g_out[pl.ds(0, rows), :] = g_last[0]
    g_out[pl.ds(rows, rows), :] = g_last[1]


def static_index(order, z, y):
    bits = {"ya": (y + y // 2) % 2, "yb": y // 2, "za": (z + z // 2) % 2, "zb": z // 2}
    return index_in(order, bits)


def sketch_call(scans, scores, number):
    time_rows, cols = scans.shape
    rank = scores.shape[1]
    piece = cols // 32
    f32 = jnp.float32
    quarter = rank // 4
    return pl.pallas_call(
        sketch_kernel,
        out_shape=(jax.ShapeDtypeStruct((rank, piece), f32), jax.ShapeDtypeStruct((rank, rank), f32)),
        in_specs=[ANY, VMEM],
        out_specs=(VMEM, VMEM),
        scratch_shapes=[
            pltpu.VMEM((4, time_rows, 4 * piece), jnp.bfloat16),
            pltpu.VMEM((4, 4, 4, quarter, piece), f32),
            pltpu.VMEM((4, 4, 4, quarter, piece), f32),
            pltpu.VMEM((4, 16, quarter, piece), f32),
            pltpu.VMEM((4, 8, quarter, piece), f32),
            pltpu.VMEM((4, 4, quarter, piece), f32),
            pltpu.VMEM((4, 2, quarter, piece), f32),
            pltpu.VMEM((4, 1, quarter, piece), f32),
            pltpu.VMEM((2, rank // 2, rank), f32),
            pltpu.VMEM((7, rank // 2, rank), f32),
            pltpu.VMEM((7, rank // 2, rank), f32),
            pltpu.VMEM((2, rank // 2, rank), f32),
            pltpu.SemaphoreType.DMA((4,)),
            pltpu.SemaphoreType.DMA((4,)),
            pltpu.SemaphoreType.DMA((4,)),
            pltpu.SemaphoreType.DMA((16,)),
            pltpu.SemaphoreType.DMA((16,)),
            pltpu.SemaphoreType.DMA((8,)),
            pltpu.SemaphoreType.DMA((8,)),
        ],
        compiler_params=pltpu.CompilerParams(
            collective_id=number, has_side_effects=True, vmem_limit_bytes=VMEM_BYTES
        ),
        name=f"sketch_{number}",
    )(scans, scores)


def gather_kernel(slice_t, out, pieces, ss, rs, sc, rc):
    place = Place()
    size = pieces.shape[3]
    bits4 = ("ya", "yb", "za", "zb")
    meet([place.sibling()] + [place.across(bit) for bit in bits4])
    own = slice_t[...].T.astype(jnp.bfloat16)
    index = [index_in(ORDERS[q], place.bits) for q in range(4)]
    for q in range(4):
        pieces[q, place.c, index[q]] = own[q * size : (q + 1) * size]
    pending = []

    def to_sibling(q, start, count, n):
        ref = pieces.at[q, place.c, pl.ds(start, count)]
        pending.append(send(ref, ref, sc.at[n * 4 + q], rc.at[n * 4 + q], place.sibling()))

    for stage in range(4):
        count = 1 << stage
        copies = []
        for q in range(4):
            bit = ORDERS[q][3 - stage]
            start = lax.div(index[q], count) * count
            ref = pieces.at[q, place.c, pl.ds(start, count)]
            n = stage * 4 + q
            copies.append(send(ref, ref, ss.at[n], rs.at[n], place.across(bit)))
        for q in range(4):
            if stage == 0:
                to_sibling(q, index[q], 1, 0)
        for q in range(4):
            copies[q].wait()
            bit = ORDERS[q][3 - stage]
            base = lax.div(index[q], 2 * count) * (2 * count)
            to_sibling(q, base + (1 - place.bits[bit]) * count, count, stage + 1)
    for copy in pending:
        copy.wait()

    def put(n, carry):
        core, zy = lax.div(n, 16), lax.rem(n, 16)
        bits = place_bits(lax.div(zy, 4), lax.rem(zy, 4))
        for q in range(4):
            at = pl.multiple_of(n * (4 * size) + q * size, 16)
            out[pl.ds(at, size), :] = pieces[q, core, index_in(ORDERS[q], bits)]
        return carry

    lax.fori_loop(0, 32, put, 0)


def gather_call(slice_t, number):
    rank, piece = slice_t.shape
    return pl.pallas_call(
        gather_kernel,
        out_shape=jax.ShapeDtypeStruct((32 * piece, rank), jnp.bfloat16),
        in_specs=[VMEM],
        out_specs=VMEM,
        scratch_shapes=[
            pltpu.VMEM((4, 2, 16, piece // 4, rank), jnp.bfloat16),
            pltpu.SemaphoreType.DMA((16,)),
            pltpu.SemaphoreType.DMA((16,)),
            pltpu.SemaphoreType.DMA((20,)),
            pltpu.SemaphoreType.DMA((20,)),
        ],
        compiler_params=pltpu.CompilerParams(
            collective_id=number, has_side_effects=True, vmem_limit_bytes=VMEM_BYTES
        ),
        name=f"gather_{number}",
    )(slice_t)


def on_device(scans, test_matrix, lengths, block_subject):
    panel = test_matrix
    for sweep in range(PASSES):
        scores = scores_call(lengths, block_subject, scans, panel, 3 * sweep)
        slice_t, gram = sketch_call(scans, scores, 3 * sweep + 1)
        factor = jnp.linalg.cholesky(gram / V)
        orthonormal_t = jax.scipy.linalg.solve_triangular(factor, slice_t, lower=True)
        panel = gather_call(orthonormal_t, 3 * sweep + 2)
    return panel.astype(jnp.float32)


def solution(mesh):
    placed = (P("subj", "vox"), P("vox", None), P(), P())
    return jax.shard_map(
        on_device, mesh=mesh, in_specs=placed, out_specs=P("vox", None), check_vma=False
    )
```

time: 501 us -> 259 us (0.52)
  waiting for transfers between devices: 318 us -> 0 us
  Pallas kernels: 0 us -> 203 us
  matrix products: 72.6 us -> 3.94 us
  blocking collectives: 35.2 us -> 0 us
  between operations: 13.2 us -> 0.14 us
    psum x4 -> x0, waiting for transfers between devices: 318 us -> none  [the longest x2 240 us: on_device(): lax.psum(lax.dot_general(scans, scores, (((0,), (0,)), ((), ())), preferr...]
    pallas_call x0 -> x6, Pallas kernels: none -> 203 us  [the longest x2 119 us: sketch_call(): pl.pallas_call(sketch_kernel, out_shape=(jax.ShapeDtypeStruct((rank, piec...]
    dot_general x6 -> x0, matrix products: 55.8 us -> none  [the longest x2 22 us: on_device(): lax.dot_general(scans, scores, (((0,), (0,)), ((), ())), preferred_elemen...]
    psum x2 -> x0, blocking collectives: 35.2 us -> none  [on_device(): summed = lax.psum(partial_scores, 'vox')]
    another operation x2, matrix products: 16.8 us -> 3.94 us  [on_device(): jax.scipy.linalg.solve_triangular(factor, slice_t, lower=True)]
    transpose x1 -> x0, local copies, waits for them, and re-layouts: 6.55 us -> none  [on_device(): jax.scipy.linalg.solve_triangular(factor, sketch.T, lower=True)]
  transfers between devices with their start and end apart: 4 -> 0, of which waited for: 4 -> 0; matrix products, arithmetic and copies ran while one was open for 0% -> 0% of each run, Pallas kernels for 0% -> 0%
where the time goes in v1:
time: 259 us
  Pallas kernels  203 us (78%)
  other arithmetic  50.1 us (19%)
  matrix products  3.94 us (2%)
    pallas_call x2, Pallas kernels, sketch_call(): pl.pallas_call(sketch_kernel, out_shape=(jax.ShapeDtypeStruct((rank, piec...  119 us
    pallas_call x2, Pallas kernels, gather_call(): pl.pallas_call(gather_kernel, out_shape=jax.ShapeDtypeStruct((32 * piece,...  48.7 us
    pallas_call x2, Pallas kernels, scores_call(): pl.pallas_call(scores_kernel, out_shape=jax.ShapeDtypeStruct((time_rows,...  34.8 us
    another operation x6, other arithmetic, on_device(): factor = jnp.linalg.cholesky(gram / V)  24.8 us
    another operation x4, other arithmetic, on_device(): jax.scipy.linalg.solve_triangular(factor, slice_t, lower=True)  20.9 us

profile of v1, /device:TPU:1, one launch (start us, length us, event | category | flops | bytes accessed | tf_op | source)
XLA Modules:
  0.0 259.1 jit_solution(3302848666638210964)
XLA Ops:
  0.0 17.8 %scores_0.1.scores = bf16[640,128]{1,0:T(8,128)(2,1)} custom-call(s32[32]{0:T(128)} %lengths.3, s32[32]{0:T(128)} %block_subject.3, bf16[640,12288]{1,0:T(8,128)(2,1)} %scans.7, bf16[12288,128]{1,0:T(8,128)(2,1)} %panel.1), custom_call_target="tpu_custom_call" | custom-call | tf_op jit(solution)/shard_map/scores_0/pallas_call | solution.py:122
  17.8 61.7 %sketch_1.1 = (f32[128,384]{1,0:T(8,128)}, f32[128,128]{1,0:T(8,128)}) custom-call(bf16[640,12288]{1,0:T(8,128)(2,1)} %scans.7, bf16[640,128]{1,0:T(8,128)(2,1)} %scores_0.1.scores), custom_call_target="tpu_custom_call" | custom-call | tf_op jit(solution)/shard_map/sketch_1/pallas_call | solution.py:244
  79.5 0.9 copy.5
  80.5 0.1 copy.6
  80.6 11.7 %cholesky.44 = f32[128,128]{1,0:T(8,128)S(1)} custom-call(f32[128,128]{1,0:T(8,128)S(1)} %fusion.7), custom_call_target="Cholesky" | custom-call | tf_op jit(solution)/shard_map/jit(cholesky)/cholesky | solution.py:349
  92.3 0.6 compare_reduce_fusion.1
  93.0 0.7 fusion
  93.6 9.8 %custom-call.6 = f32[1,128,128]{1,2,0:T(8,128)S(1)} custom-call(f32[1,128,128]{2,1,0:T(8,128)S(1)} %fusion), custom_call_target="InvertDiagBlocksLowerTriangular" | custom-call | tf_op jit(solution)/shard_map/jit(_solve_triangular)/triangular_solve | solution.py:350
  103.4 2.0 fusion.5.slice_t
  105.4 24.3 %gather_2.1.panel = bf16[12288,128]{1,0:T(8,128)(2,1)} custom-call(f32[128,384]{1,0:T(8,128)} %fusion.5.slice_t), custom_call_target="tpu_custom_call" | custom-call | tf_op jit(solution)/shard_map/gather_2/pallas_call | solution.py:325
  129.7 16.9 %scores_3.1.scores = bf16[640,128]{1,0:T(8,128)(2,1)} custom-call(s32[32]{0:T(128)} %lengths.3, s32[32]{0:T(128)} %block_subject.3, bf16[640,12288]{1,0:T(8,128)(2,1)} %scans.7, bf16[12288,128]{1,0:T(8,128)(2,1)} %gather_2.1.panel), custom_call_target="tpu_custom_call" | custom-call | tf_op jit(solution)/shard_map/scores_3/pallas_call | solution.py:122
  146.7 57.8 %sketch_4.1 = (f32[128,384]{1,0:T(8,128)}, f32[128,128]{1,0:T(8,128)}) custom-call(bf16[640,12288]{1,0:T(8,128)(2,1)} %scans.7, bf16[640,128]{1,0:T(8,128)(2,1)} %scores_3.1.scores), custom_call_target="tpu_custom_call" | custom-call | tf_op jit(solution)/shard_map/sketch_4/pallas_call | solution.py:244
  204.5 0.9 copy.7
  205.4 0.1 copy.8
  205.5 11.7 %cholesky.55 = f32[128,128]{1,0:T(8,128)S(1)} custom-call(f32[128,128]{1,0:T(8,128)S(1)} %fusion.4), custom_call_target="Cholesky" | custom-call | tf_op jit(solution)/shard_map/jit(cholesky)/cholesky | solution.py:349
  217.3 0.6 compare_reduce_fusion
  217.9 0.7 fusion.1
  218.6 9.8 %custom-call.7 = f32[1,128,128]{1,2,0:T(8,128)S(1)} custom-call(f32[1,128,128]{2,1,0:T(8,128)S(1)} %fusion.1), custom_call_target="InvertDiagBlocksLowerTriangular" | custom-call | tf_op jit(solution)/shard_map/jit(_solve_triangular)/triangular_solve | solution.py:350
  228.4 2.0 fusion.2.slice_t
  230.4 24.3 %gather_5.1 = bf16[12288,128]{1,0:T(8,128)(2,1)} custom-call(f32[128,384]{1,0:T(8,128)} %fusion.2.slice_t), custom_call_target="tpu_custom_call" | custom-call | tf_op jit(solution)/shard_map/gather_5/pallas_call | solution.py:325
  254.7 4.3 %convert_element_type.3 = f32[12288,128]{1,0:T(8,128)} convert(bf16[12288,128]{1,0:T(8,128)(2,1)} %gather_5.1) | non-fusion elementwise | flops 1572864 | bytes 9437184 | tf_op jit(solution)/shard_map/convert_element_type | solution.py:352
  (6 shorter events, 0.1 us)

commit v2 on v1

--- a/solution.py
+++ b/solution.py
@@ -18,8 +18,8 @@
 
 
 def ring_bits(i):
-    b = lax.div(i, 2)
-    return lax.rem(i + b, 2), b
+    b = i // 2 if isinstance(i, int) else lax.div(i, 2)
+    return (i + b) % 2 if isinstance(i, int) else lax.rem(i + b, 2), b
 
 
 def flip_a(i):
@@ -61,11 +61,15 @@
     return 8 * bits[order[0]] + 4 * bits[order[1]] + 2 * bits[order[2]] + bits[order[3]]
 
 
-def meet(devices):
+def greet(devices):
     barrier = pltpu.get_barrier_semaphore()
     for device in devices:
         pl.semaphore_signal(barrier, inc=1, device_id=device, device_id_type=MESH)
-    pl.semaphore_wait(barrier, len(devices))
+    return barrier, len(devices)
+
+
+def meet(devices):
+    pl.semaphore_wait(*greet(devices))
 
 
 def send(src, dst, send_sem, recv_sem, device):
@@ -142,8 +146,15 @@
     )(lengths, block_subject, scans, panel)
 
 
+def flipped(order, bits, m):
+    index = 0
+    for weight, bit in zip((8, 4, 2, 1), order):
+        index = index + weight * (1 - bits[bit] if m & weight else bits[bit])
+    return index
+
+
 def sketch_kernel(
-    scans, scores, z_out, g_out, held, away, arrived, mine, in1, in2, in3, in4, g_part, g_in, g_sum, g_last,
+    scans, scores, z_out, g_out, held, away, arrived, mine, inbox, g_part, g_in, g_sum, g_last,
     load_sem, sc, rc, ss, rs, sg, rg,
 ):
     place = Place()
@@ -151,63 +162,70 @@
     rank, piece = z_out.shape
     quarter = rank // 4
     slots = held.shape[0]
-
-    def block_of(t):
-        core = lax.rem(place.c + 1 + t // 4, 2)
-        return core * 16 + (t % 4) * 4
+    z_far = (flip_a(flip_b(place.z)), flip_a(place.z), flip_b(place.z), place.z)
+    z_flips = ({"za", "zb"}, {"za"}, {"zb"}, set())
+    steps = [(1, 0), (1, 1), (0, 0), (1, 2), (0, 1), (1, 3), (0, 2), (0, 3)]
 
     def load(t):
-        start = pl.multiple_of(block_of(t) * piece, width)
+        away_side, k = steps[t]
+        core = 1 - place.c if away_side else place.c
+        start = pl.multiple_of((core * 16 + z_far[k] * 4) * piece, width)
         return pltpu.make_async_copy(scans.at[:, pl.ds(start, width)], held.at[t % slots], load_sem.at[t % slots])
 
     for t in range(slots - 1):
         load(t).start()
-    bits7 = ("xa", "xb", "ya", "yb", "za", "zb")
-    meet([place.sibling()] + [place.across(bit) for bit in bits7])
+    bits6 = ("xa", "xb", "ya", "yb", "za", "zb")
+    meet([place.sibling()] + [place.across(bit) for bit in bits6])
     left = scores[...].T
-    core_copies = []
+    core_copies = {}
+    copies = []
+    at = [[flipped(ORDERS[q], place.bits, m) for m in range(16)] for q in range(4)]
+
+    def pass_on(q, m):
+        bit = ORDERS[q][{8: 0, 4: 1, 2: 2, 1: 3}[1 << (m.bit_length() - 1)]]
+        copies.append(send(mine.at[q, at[q][m]], inbox.at[q, m], ss.at[q, m], rs.at[q, m], place.across(bit)))
+
+    def take(q, m, weight):
+        ref = inbox.at[q, weight | m]
+        pltpu.make_async_copy(ref, ref, rs.at[q, weight | m]).wait()
+        return inbox[q, weight | m]
+
     for t in range(8):
         if t + slots - 1 < 8:
             load(t + slots - 1).start()
         load(t).wait()
-        z = t % 4
+        away_side, k = steps[t]
         block = jnp.dot(left, held[t % slots], preferred_element_type=jnp.float32)
-        if t >= 4:
-            core_copies[z].wait()
+        if not away_side:
+            core_copies[k].wait()
         for y in range(4):
-            bits = place_bits(jnp.int32(z), jnp.int32(y))
+            bits = place_bits(z_far[k], y)
             for q in range(4):
                 value = block[q * quarter : (q + 1) * quarter, y * piece : (y + 1) * piece]
-                if t < 4:
-                    away[z, q, y] = value
+                if away_side:
+                    away[k, q, y] = value
                 else:
-                    mine[q, static_index(ORDERS[q], z, y)] = value + arrived[z, q, y]
-        if t < 4:
-            core_copies.append(send(away.at[z], arrived.at[z], sc.at[z], rc.at[z], place.sibling()))
-
-    offset = [jnp.int32(0)] * 4
-    for stage, inbox in enumerate((in1, in2, in3, in4)):
-        half = 8 >> stage
-        copies = []
+                    mine[q, index_in(ORDERS[q], bits)] = value + arrived[k, q, y]
+        if away_side:
+            core_copies[k] = send(away.at[k], arrived.at[k], sc.at[k], rc.at[k], place.sibling())
+            continue
+        for m in range(15, 7, -1):
+            for q in range(4):
+                flips = {bit for weight, bit in zip((8, 4, 2, 1), ORDERS[q]) if m & weight}
+                if flips & {"za", "zb"} == z_flips[k]:
+                    pass_on(q, m)
+
+    for m in range(7, -1, -1):
         for q in range(4):
-            bit = ORDERS[q][stage]
-            there = offset[q] + (1 - place.bits[bit]) * half
-            n = stage * 4 + q
-            copies.append(
-                send(mine.at[q, pl.ds(there, half)], inbox.at[q], ss.at[n], rs.at[n], place.across(bit))
-            )
-            offset[q] = offset[q] + place.bits[bit] * half
-        for q in range(4):
-            copies[q].wait()
-
-            def add(i, carry, q=q, inbox=inbox):
-                at = offset[q] + i
-                mine[q, at] = mine[q, at] + inbox[q, i]
-                return carry
-
-            lax.fori_loop(0, half, add, 0)
-    for q in range(4):
-        z_out[pl.ds(q * quarter, quarter), :] = mine[q, offset[q]]
+            value = mine[q, at[q][m]]
+            for weight in (8, 4, 2, 1):
+                if weight > m:
+                    value = value + take(q, m, weight)
+            if m:
+                mine[q, at[q][m]] = value
+                pass_on(q, m)
+            else:
+                z_out[q * quarter : (q + 1) * quarter, :] = value
 
     own = z_out[...]
     gram = lax.dot_general(
@@ -217,9 +235,11 @@
     g_part[0] = gram[:rows]
     g_part[1] = gram[rows:]
     copy = send(g_part.at[1 - place.c], g_in.at[0], sg.at[0], rg.at[0], place.sibling())
+    for done in copies:
+        done.wait_send()
     copy.wait()
     g_sum[0] = g_part[place.c] + g_in[0]
-    for n, bit in enumerate(bits7):
+    for n, bit in enumerate(bits6):
         copy = send(g_sum.at[n], g_in.at[n + 1], sg.at[n + 1], rg.at[n + 1], place.across(bit))
         copy.wait()
         g_sum[n + 1] = g_sum[n] + g_in[n + 1]
@@ -228,11 +248,6 @@
     copy.wait()
     g_out[pl.ds(0, rows), :] = g_last[0]
     g_out[pl.ds(rows, rows), :] = g_last[1]
-
-
-def static_index(order, z, y):
-    bits = {"ya": (y + y // 2) % 2, "yb": y // 2, "za": (z + z // 2) % 2, "zb": z // 2}
-    return index_in(order, bits)
 
 
 def sketch_call(scans, scores, number):
@@ -251,10 +266,7 @@
             pltpu.VMEM((4, 4, 4, quarter, piece), f32),
             pltpu.VMEM((4, 4, 4, quarter, piece), f32),
             pltpu.VMEM((4, 16, quarter, piece), f32),
-            pltpu.VMEM((4, 8, quarter, piece), f32),
-            pltpu.VMEM((4, 4, quarter, piece), f32),
-            pltpu.VMEM((4, 2, quarter, piece), f32),
-            pltpu.VMEM((4, 1, quarter, piece), f32),
+            pltpu.VMEM((4, 16, quarter, piece), f32),
             pltpu.VMEM((2, rank // 2, rank), f32),
             pltpu.VMEM((7, rank // 2, rank), f32),
             pltpu.VMEM((7, rank // 2, rank), f32),
@@ -262,8 +274,8 @@
             pltpu.SemaphoreType.DMA((4,)),
             pltpu.SemaphoreType.DMA((4,)),
             pltpu.SemaphoreType.DMA((4,)),
-            pltpu.SemaphoreType.DMA((16,)),
-            pltpu.SemaphoreType.DMA((16,)),
+            pltpu.SemaphoreType.DMA((4, 16)),
+            pltpu.SemaphoreType.DMA((4, 16)),
             pltpu.SemaphoreType.DMA((8,)),
             pltpu.SemaphoreType.DMA((8,)),
         ],
@@ -274,71 +286,100 @@
     )(scans, scores)
 
 
-def gather_kernel(slice_t, out, pieces, ss, rs, sc, rc):
+def inverse_factor(gram):
+    n, width = gram.shape[0], 8
+    row, col = (lax.broadcasted_iota(jnp.int32, (n, n), d) for d in (0, 1))
+    left, right = gram, (row == col).astype(jnp.float32)
+    place = lax.broadcasted_iota(jnp.int32, (width, n), 0)
+    done = []
+    for k in range(0, n, width):
+        columns = [jnp.broadcast_to(left[:, k + j : k + j + 1], left.shape) for j in range(width)]
+        heads, tails = [c[:width] for c in columns], [c[width:] for c in columns]
+        left_head, right_head = left[:width], right[:width]
+        left, right = left[width:], right[width:]
+        pivots = jnp.zeros((width, n), jnp.float32)
+        for j in range(width):
+            pivot = heads[j][j : j + 1]
+            over = 1.0 / pivot
+            pivots = jnp.where(place == j, jnp.broadcast_to(pivot, (width, n)), pivots)
+            head = jnp.where(place > j, heads[j] * over, 0.0)
+            left_row, right_row = left_head[j : j + 1], right_head[j : j + 1]
+            if k + width < n:
+                tail = tails[j] * over
+                left, right = left - tail * left_row, right - tail * right_row
+            for i in range(j + 1, width):
+                factor = heads[j][i : i + 1]
+                heads[i] = heads[i] - head * factor
+                if k + width < n:
+                    tails[i] = tails[i] - tail * factor
+            left_head, right_head = left_head - head * left_row, right_head - head * right_row
+        done.append(right_head * lax.rsqrt(pivots))
+    return jnp.concatenate(done, 0)
+
+
+def gather_kernel(slice_t, gram, out, pieces, ss, rs, sc, rc):
     place = Place()
     size = pieces.shape[3]
-    bits4 = ("ya", "yb", "za", "zb")
-    meet([place.sibling()] + [place.across(bit) for bit in bits4])
-    own = slice_t[...].T.astype(jnp.bfloat16)
-    index = [index_in(ORDERS[q], place.bits) for q in range(4)]
+    greeted = greet([place.sibling()] + [place.across(bit) for bit in ("ya", "yb", "za", "zb")])
+    inverse = inverse_factor(gram[...] / V)
+    own = jnp.dot(inverse, slice_t[...], precision=lax.Precision.HIGHEST, preferred_element_type=jnp.float32)
+    own = own.T.astype(jnp.bfloat16)
+    at = [[flipped(ORDERS[q], place.bits, m) for m in range(16)] for q in range(4)]
     for q in range(4):
-        pieces[q, place.c, index[q]] = own[q * size : (q + 1) * size]
-    pending = []
-
-    def to_sibling(q, start, count, n):
-        ref = pieces.at[q, place.c, pl.ds(start, count)]
-        pending.append(send(ref, ref, sc.at[n * 4 + q], rc.at[n * 4 + q], place.sibling()))
-
-    for stage in range(4):
-        count = 1 << stage
-        copies = []
+        pieces[q, place.c, at[q][0]] = own[q * size : (q + 1) * size]
+    pl.semaphore_wait(*greeted)
+    copies = []
+
+    def pass_on(q, m):
+        ref = pieces.at[q, place.c, at[q][m]]
+        for weight, bit in ((1, 3), (2, 2), (4, 1), (8, 0)):
+            if weight > m:
+                n = weight | m
+                copies.append(send(ref, ref, ss.at[q, n], rs.at[q, n], place.across(ORDERS[q][bit])))
+
+    def to_sibling(q, m):
+        ref = pieces.at[q, place.c, at[q][m]]
+        copies.append(send(ref, ref, sc.at[q, m], rc.at[q, m], place.sibling()))
+
+    for m in (0, 1, 2, 4, 3, 5, 6, 7, 8, 9, 10, 12, 11, 13, 14, 15):
         for q in range(4):
-            bit = ORDERS[q][3 - stage]
-            start = lax.div(index[q], count) * count
-            ref = pieces.at[q, place.c, pl.ds(start, count)]
-            n = stage * 4 + q
-            copies.append(send(ref, ref, ss.at[n], rs.at[n], place.across(bit)))
-        for q in range(4):
-            if stage == 0:
-                to_sibling(q, index[q], 1, 0)
-        for q in range(4):
-            copies[q].wait()
-            bit = ORDERS[q][3 - stage]
-            base = lax.div(index[q], 2 * count) * (2 * count)
-            to_sibling(q, base + (1 - place.bits[bit]) * count, count, stage + 1)
-    for copy in pending:
-        copy.wait()
+            if m:
+                ref = pieces.at[q, place.c, at[q][m]]
+                pltpu.make_async_copy(ref, ref, rs.at[q, m]).wait()
+            pass_on(q, m)
+            to_sibling(q, m)
+    for q in range(4):
+        for m in range(16):
+            ref = pieces.at[q, 1 - place.c, at[q][m]]
+            pltpu.make_async_copy(ref, ref, rc.at[q, m]).wait()
+    for copy in copies:
+        copy.wait_send()
 
     def put(n, carry):
         core, zy = lax.div(n, 16), lax.rem(n, 16)
         bits = place_bits(lax.div(zy, 4), lax.rem(zy, 4))
         for q in range(4):
-            at = pl.multiple_of(n * (4 * size) + q * size, 16)
-            out[pl.ds(at, size), :] = pieces[q, core, index_in(ORDERS[q], bits)]
+            start = pl.multiple_of(n * (4 * size) + q * size, 16)
+            out[pl.ds(start, size), :] = pieces[q, core, index_in(ORDERS[q], bits)]
         return carry
 
     lax.fori_loop(0, 32, put, 0)
 
 
-def gather_call(slice_t, number):
+def gather_call(slice_t, gram, number):
     rank, piece = slice_t.shape
     return pl.pallas_call(
         gather_kernel,
         out_shape=jax.ShapeDtypeStruct((32 * piece, rank), jnp.bfloat16),
-        in_specs=[VMEM],
+        in_specs=[VMEM, VMEM],
         out_specs=VMEM,
-        scratch_shapes=[
-            pltpu.VMEM((4, 2, 16, piece // 4, rank), jnp.bfloat16),
-            pltpu.SemaphoreType.DMA((16,)),
-            pltpu.SemaphoreType.DMA((16,)),
-            pltpu.SemaphoreType.DMA((20,)),
-            pltpu.SemaphoreType.DMA((20,)),
-        ],
+        scratch_shapes=[pltpu.VMEM((4, 2, 16, piece // 4, rank), jnp.bfloat16)]
+        + [pltpu.SemaphoreType.DMA((4, 16))] * 4,
         compiler_params=pltpu.CompilerParams(
             collective_id=number, has_side_effects=True, vmem_limit_bytes=VMEM_BYTES
         ),
         name=f"gather_{number}",
-    )(slice_t)
+    )(slice_t, gram)
 
 
 def on_device(scans, test_matrix, lengths, block_subject):
@@ -346,9 +387,7 @@
     for sweep in range(PASSES):
         scores = scores_call(lengths, block_subject, scans, panel, 3 * sweep)
         slice_t, gram = sketch_call(scans, scores, 3 * sweep + 1)
-        factor = jnp.linalg.cholesky(gram / V)
-        orthonormal_t = jax.scipy.linalg.solve_triangular(factor, slice_t, lower=True)
-        panel = gather_call(orthonormal_t, 3 * sweep + 2)
+        panel = gather_call(slice_t, gram, 3 * sweep + 2)
     return panel.astype(jnp.float32)
 
 

time: 259 us -> 194 us (0.75)
  other arithmetic: 50.1 us -> 4.32 us
  Pallas kernels: 203 us -> 190 us
  matrix products: 3.94 us -> 0 us
    another operation x10 -> x0, other arithmetic: 45.7 us -> none  [the longest x6 24.8 us: on_device(): factor = jnp.linalg.cholesky(gram / V)]
    pallas_call x2, Pallas kernels: 119 us -> 103 us  [sketch_call(): pl.pallas_call(sketch_kernel, out_shape=(jax.ShapeDtypeStruct((rank, piec...]
    another operation x2 -> x0, matrix products: 3.94 us -> none  [on_device(): jax.scipy.linalg.solve_triangular(factor, slice_t, lower=True)]
where the time goes in v2:
time: 194 us
  Pallas kernels  190 us (98%)
  other arithmetic  4.32 us (2%)
    pallas_call x2, Pallas kernels, sketch_call(): pl.pallas_call(sketch_kernel, out_shape=(jax.ShapeDtypeStruct((rank, piec...  103 us
    pallas_call x2, Pallas kernels, gather_call(): pl.pallas_call(gather_kernel, out_shape=jax.ShapeDtypeStruct((32 * piece,...  51.2 us
    pallas_call x2, Pallas kernels, scores_call(): pl.pallas_call(scores_kernel, out_shape=jax.ShapeDtypeStruct((time_rows,...  35.6 us
    convert_element_type x1, other arithmetic, on_device(): return panel.astype(jnp.float32)  4.32 us

profile of v2, /device:TPU:1, one launch (start us, length us, event | category | flops | bytes accessed | tf_op | source)
XLA Modules:
  0.0 194.0 jit_solution(9481853431370084324)
XLA Ops:
  0.0 17.8 %scores_0.1.scores = bf16[640,128]{1,0:T(8,128)(2,1)} custom-call(s32[32]{0:T(128)} %lengths.3, s32[32]{0:T(128)} %block_subject.3, bf16[640,12288]{1,0:T(8,128)(2,1)} %scans.7, bf16[12288,128]{1,0:T(8,128)(2,1)} %panel.1), custom_call_target="tpu_custom_call" | custom-call | tf_op jit(solution)/shard_map/scores_0/pallas_call | solution.py:126
  17.8 53.8 %sketch_1.1 = (f32[128,384]{1,0:T(8,128)}, f32[128,128]{1,0:T(8,128)}) custom-call(bf16[640,12288]{1,0:T(8,128)(2,1)} %scans.7, bf16[640,128]{1,0:T(8,128)(2,1)} %scores_0.1.scores), custom_call_target="tpu_custom_call" | custom-call | tf_op jit(solution)/shard_map/sketch_1/pallas_call | solution.py:259
  71.7 25.5 %gather_2.1.panel = bf16[12288,128]{1,0:T(8,128)(2,1)} custom-call(f32[128,384]{1,0:T(8,128)} %get-tuple-element.9.slice_t, f32[128,128]{1,0:T(8,128)} %get-tuple-element.10.gram), custom_call_target="tpu_custom_call" | custom-call | tf_op jit(solution)/shard_map/gather_2/pallas_call | solution.py:371
  97.1 17.8 %scores_3.1.scores = bf16[640,128]{1,0:T(8,128)(2,1)} custom-call(s32[32]{0:T(128)} %lengths.3, s32[32]{0:T(128)} %block_subject.3, bf16[640,12288]{1,0:T(8,128)(2,1)} %scans.7, bf16[12288,128]{1,0:T(8,128)(2,1)} %gather_2.1.panel), custom_call_target="tpu_custom_call" | custom-call | tf_op jit(solution)/shard_map/scores_3/pallas_call | solution.py:126
  115.0 49.0 %sketch_4.1 = (f32[128,384]{1,0:T(8,128)}, f32[128,128]{1,0:T(8,128)}) custom-call(bf16[640,12288]{1,0:T(8,128)(2,1)} %scans.7, bf16[640,128]{1,0:T(8,128)(2,1)} %scores_3.1.scores), custom_call_target="tpu_custom_call" | custom-call | tf_op jit(solution)/shard_map/sketch_4/pallas_call | solution.py:259
  163.9 25.7 %gather_5.1 = bf16[12288,128]{1,0:T(8,128)(2,1)} custom-call(f32[128,384]{1,0:T(8,128)} %get-tuple-element.11.slice_t, f32[128,128]{1,0:T(8,128)} %get-tuple-element.12.gram), custom_call_target="tpu_custom_call" | custom-call | tf_op jit(solution)/shard_map/gather_5/pallas_call | solution.py:371
  189.7 4.3 %convert_element_type.3 = f32[12288,128]{1,0:T(8,128)} convert(bf16[12288,128]{1,0:T(8,128)(2,1)} %gather_5.1) | non-fusion elementwise | flops 1572864 | bytes 9437184 | tf_op jit(solution)/shard_map/convert_element_type | solution.py:391

commit v3 on v0

v3 whole, which is shorter than its diff:
```python
import functools

import jax
import jax.numpy as jnp
from jax import lax
from jax.experimental import pallas as pl
from jax.experimental.pallas import tpu as pltpu
from jax.sharding import PartitionSpec as P

V = 49152
PASSES = 2
MESH = pl.DeviceIdType.MESH
VMEM_BYTES = 62 * 2**20
ANY = pl.BlockSpec(memory_space=pl.ANY)
VMEM = pl.BlockSpec(memory_space=pltpu.VMEM)
SMEM = pl.BlockSpec(memory_space=pltpu.SMEM)
DMA = pltpu.SemaphoreType.DMA
f32, bf16 = jnp.float32, jnp.bfloat16
ORDERS = (("ya", "yb", "za", "zb"), ("yb", "ya", "zb", "za"), ("za", "zb", "ya", "yb"), ("zb", "za", "yb", "ya"))
WEIGHTS = (8, 4, 2, 1)


def flip_a(i):
    return i + 1 - 2 * lax.rem(i, 2)


def flip_b(i):
    return 3 - i


class Place:
    def __init__(self):
        here = lax.axis_index("subj")
        self.z, self.y, self.c = lax.div(here, 8), lax.rem(lax.div(here, 2), 4), lax.rem(here, 2)
        self.x = lax.axis_index("vox")

    def flipped(self, bits):
        z, y = self.z, self.y
        z = flip_a(z) if "za" in bits else z
        z = flip_b(z) if "zb" in bits else z
        y = flip_a(y) if "ya" in bits else y
        y = flip_b(y) if "yb" in bits else y
        return z, y

    def across(self, bit):
        z, y = self.flipped((bit,))
        return {"subj": z * 8 + y * 2 + self.c}

    def sibling(self):
        return {"subj": self.z * 8 + self.y * 2 + 1 - self.c}

    def in_plane(self, step):
        z, y = lax.rem(self.z + step // 4, 4), lax.rem(self.y + step % 4, 4)
        return z * 4 + y, {"subj": z * 8 + y * 2 + self.c}

    def along_x(self, step, other_core):
        x = lax.rem(self.x + step, 4)
        c = 1 - self.c if other_core else self.c
        return x * 2 + c, {"subj": self.z * 8 + self.y * 2 + c, "vox": x}


def flips_of(order, m):
    return tuple(bit for weight, bit in zip(WEIGHTS, order) if m & weight)


def pair_index(place, q, m):
    z, y = place.flipped(flips_of(ORDERS[q], m))
    return z * 4 + y


def greet(devices):
    barrier = pltpu.get_barrier_semaphore()
    for device in devices:
        pl.semaphore_signal(barrier, inc=1, device_id=device, device_id_type=MESH)
    return barrier, len(devices)


def send(src, dst, send_sem, recv_sem, device):
    copy = pltpu.make_async_remote_copy(
        src_ref=src, dst_ref=dst, send_sem=send_sem, recv_sem=recv_sem, device_id=device, device_id_type=MESH
    )
    copy.start()
    return copy


def landed(ref, sem):
    pltpu.make_async_copy(ref, ref, sem).wait()


def inverse_factor(gram):
    n, width = gram.shape[0], 8
    row, col = (lax.broadcasted_iota(jnp.int32, (n, n), d) for d in (0, 1))
    left, right = gram, (row == col).astype(jnp.float32)
    place = lax.broadcasted_iota(jnp.int32, (width, n), 0)
    done = []
    for k in range(0, n, width):
        columns = [jnp.broadcast_to(left[:, k + j : k + j + 1], left.shape) for j in range(width)]
        heads, tails = [c[:width] for c in columns], [c[width:] for c in columns]
        left_head, right_head = left[:width], right[:width]
        left, right = left[width:], right[width:]
        pivots = jnp.zeros((width, n), jnp.float32)
        for j in range(width):
            pivot = heads[j][j : j + 1]
            over = 1.0 / pivot
            pivots = jnp.where(place == j, jnp.broadcast_to(pivot, (width, n)), pivots)
            head = jnp.where(place > j, heads[j] * over, 0.0)
            left_row, right_row = left_head[j : j + 1], right_head[j : j + 1]
            if k + width < n:
                tail = tails[j] * over
                left, right = left - tail * left_row, right - tail * right_row
            for i in range(j + 1, width):
                factor = heads[j][i : i + 1]
                heads[i] = heads[i] - head * factor
                if k + width < n:
                    tails[i] = tails[i] - tail * factor
            left_head, right_head = left_head - head * left_row, right_head - head * right_row
        done.append(right_head * lax.rsqrt(pivots))
    return jnp.concatenate(done, 0)


def normalised(slice_t, gram):
    inverse = inverse_factor(gram[...] / V)
    own = jnp.dot(inverse, slice_t[...], precision=lax.Precision.HIGHEST, preferred_element_type=f32)
    return own.T.astype(bf16)


def own_rows_in(place, own, panel):
    size = own.shape[0] // 4
    chunk = 4 * size

    def rows(core, q, m):
        start = (core * 16 + pair_index(place, q, m)) * chunk + q * size
        return panel.at[pl.ds(pl.multiple_of(start, 32), size)]

    for q in range(4):
        rows(place.c, q, 0)[...] = own[q * size : (q + 1) * size]
    return rows


def exchange_panel(place, rows, ss, rs, sc, rc):
    copies = []
    for m in (0, 1, 2, 4, 3, 5, 6, 7, 8, 9, 10, 12, 11, 13, 14, 15):
        for q in range(4):
            ref = rows(place.c, q, m)
            if m:
                landed(ref, rs.at[q, m])
            for weight, bit in ((1, 3), (2, 2), (4, 1), (8, 0)):
                if weight > m:
                    n = weight | m
                    copies.append(send(ref, ref, ss.at[q, n], rs.at[q, n], place.across(ORDERS[q][bit])))
            copies.append(send(ref, ref, sc.at[q, m], rc.at[q, m], place.sibling()))
    for q in range(4):
        for m in range(16):
            landed(rows(1 - place.c, q, m), rc.at[q, m])
    for copy in copies:
        copy.wait_send()


def panel_kernel(slice_t, gram, panel, ss, rs, sc, rc):
    place = Place()
    greeted = greet([place.sibling()] + [place.across(bit) for bit in ORDERS[0]])
    rows = own_rows_in(place, normalised(slice_t, gram), panel)
    pl.semaphore_wait(*greeted)
    exchange_panel(place, rows, ss, rs, sc, rc)


def panel_call(slice_t, gram, number):
    rank, piece = slice_t.shape
    return pl.pallas_call(
        panel_kernel,
        out_shape=jax.ShapeDtypeStruct((32 * piece, rank), bf16),
        in_specs=[VMEM, VMEM],
        out_specs=VMEM,
        scratch_shapes=[DMA((4, 16))] * 4,
        compiler_params=pltpu.CompilerParams(
            collective_id=number, has_side_effects=True, vmem_limit_bytes=VMEM_BYTES
        ),
        name=f"panel_{number}",
    )(slice_t, gram)


def sweep_kernel(first, *refs):
    lengths, block_subject, scans = refs[:3]
    if first:
        panel_in, *refs = refs[3:]
        panel = panel_in
    else:
        slice_in, gram_in, *refs = refs[3:]
        panel, sp, rp, sq, rq = refs[-5:]
        refs = refs[:-5]
    (
        z_out, g_out, held, part, got, full, away, arrived, mine, inbox, g_part, g_in, g_side, g_full,
        load_sem, s1, r1, s2, r2, sc, rc, ss, rs, sg, rg, sh, rh, si, ri,
    ) = refs
    place = Place()
    x = place.x
    rows = part.shape[1]
    owners = [lax.rem(x + step, 4) for step in (2, 1, 3, 0)]
    plane = [place.in_plane(step) for step in range(16)]
    beside = [(dx, dc, *place.along_x(dx, dc)) for dx in range(4) for dc in (0, 1) if dx or dc]
    greeted = greet([device for _, device in plane[1:]] + [device for *_, device in beside])

    def load(n):
        half = rows // 2
        at = pl.ds(pl.multiple_of(owners[n // 2] * rows + n % 2 * half, half), half)
        return pltpu.make_async_copy(scans.at[at], held.at[at], load_sem.at[n])

    ahead = 3
    for n in range(ahead if first else 8):
        load(n).start()
    if not first:
        slices = own_rows_in(place, normalised(slice_in, gram_in), panel)
        pl.semaphore_wait(*greeted)
        exchange_panel(place, slices, sp, rp, sq, rq)

    tile = 3072
    copies = []
    for t in range(4):
        for n in (2 * t, 2 * t + 1):
            if first and n + ahead < 8:
                load(n + ahead).start()
            load(n).wait()

        def add(k, acc, t=t):
            at = pl.multiple_of(k * tile, tile)
            own_rows = pl.ds(pl.multiple_of(owners[t] * rows, rows), rows)
            return acc + jnp.dot(held[own_rows, pl.ds(at, tile)], panel[pl.ds(at, tile), :], preferred_element_type=f32)

        part[t] = lax.fori_loop(0, panel.shape[0] // tile, add, jnp.zeros(part.shape[1:], f32))
        if t == 0 and first:
            pl.semaphore_wait(*greeted)
        if t < 3:
            copies.append(send(part.at[t], got.at[t], s1.at[t], r1.at[t], {"vox": owners[t]}))
    total = part[3]
    for t in range(3):
        copies[t].wait()
        total = total + got[t]
    length = lengths[block_subject[lax.axis_index("subj")]]
    time_ids = x * rows + lax.broadcasted_iota(jnp.int32, total.shape, 0)
    full[x] = jnp.where(time_ids < length, total, f32(0.0)).astype(bf16)
    copies = [send(full.at[x], full.at[x], s2.at[t], r2.at[t], {"vox": owners[t]}) for t in range(3)]
    for copy in copies:
        copy.wait()
    left = jnp.concatenate([full[i] for i in range(4)], 0).T

    rank, piece = z_out.shape
    quarter, width = rank // 4, 4 * piece
    z_flips = (("za", "zb"), ("za",), ("zb",), ())
    z_far = [place.flipped(flips)[0] for flips in z_flips]
    copies, core_copies = [], {}
    pair = [[pair_index(place, q, m) for m in range(16)] for q in range(4)]

    def pass_on(q, m):
        bit = ORDERS[q][4 - m.bit_length()]
        copies.append(send(mine.at[q, pair[q][m]], inbox.at[q, m], ss.at[q, m], rs.at[q, m], place.across(bit)))

    for away_side, k in ((1, 0), (1, 1), (0, 0), (1, 2), (0, 1), (1, 3), (0, 2), (0, 3)):
        core = 1 - place.c if away_side else place.c
        start = pl.multiple_of((core * 16 + z_far[k] * 4) * piece, width)
        block = jnp.dot(left, held[:, pl.ds(start, width)], preferred_element_type=f32)
        if not away_side:
            core_copies[k].wait()
        for y in range(4):
            for q in range(4):
                value = block[q * quarter : (q + 1) * quarter, y * piece : (y + 1) * piece]
                if away_side:
                    away[k, q, y] = value
                else:
                    mine[q, z_far[k] * 4 + y] = value + arrived[k, q, y]
        if away_side:
            core_copies[k] = send(away.at[k], arrived.at[k], sc.at[k], rc.at[k], place.sibling())
            continue
        for m in range(15, 7, -1):
            for q in range(4):
                if tuple(bit for bit in ("za", "zb") if bit in flips_of(ORDERS[q], m)) == z_flips[k]:
                    pass_on(q, m)

    for m in range(7, -1, -1):
        for q in range(4):
            value = mine[q, pair[q][m]]
            for weight in WEIGHTS:
                if weight > m:
                    landed(inbox.at[q, weight | m], rs.at[q, weight | m])
                    value = value + inbox[q, weight | m]
            if m:
                mine[q, pair[q][m]] = value
                pass_on(q, m)
            else:
                z_out[q * quarter : (q + 1) * quarter, :] = value

    own = z_out[...]
    gram = lax.dot_general(own, own, (((1,), (1,)), ((), ())), precision=lax.Precision.HIGHEST, preferred_element_type=f32)
    for p in range(16):
        g_part[p] = gram[8 * p : 8 * p + 8]
    here = plane[0][0]
    moved = [send(g_part.at[plane[r][0]], g_in.at[r], sg.at[r], rg.at[r], plane[r][1]) for r in range(1, 16)]
    for copy in copies:
        copy.wait_send()
    total = g_part[here]
    for r in range(1, 16):
        moved[r - 1].wait()
        total = total + g_in[r]
    me = x * 2 + place.c
    g_side[me] = total
    moved = [send(g_side.at[me], g_side.at[me], sh.at[n], rh.at[me], to[3]) for n, to in enumerate(beside)]
    for copy in moved:
        copy.wait_send()
    for to in beside:
        landed(g_side.at[to[2]], rh.at[to[2]])
    total = g_side[0]
    for n in range(1, 8):
        total = total + g_side[n]
    g_full[here] = total
    moved = [send(g_full.at[here], g_full.at[here], si.at[r], ri.at[r], plane[r][1]) for r in range(1, 16)]
    for copy in moved:
        copy.wait()
    for p in range(16):
        g_out[8 * p : 8 * p + 8, :] = g_full[p]


def sweep_call(lengths, block_subject, scans, panel, number):
    first = len(panel) == 1
    time_rows, cols = scans.shape
    rank = 128
    piece, quarter, rows = cols // 32, rank // 4, time_rows // 4
    scratch = [
        pltpu.VMEM((time_rows, cols), bf16),
        pltpu.VMEM((4, rows, rank), f32),
        pltpu.VMEM((3, rows, rank), f32),
        pltpu.VMEM((4, rows, rank), bf16),
        pltpu.VMEM((4, 4, 4, quarter, piece), f32),
        pltpu.VMEM((4, 4, 4, quarter, piece), f32),
        pltpu.VMEM((4, 16, quarter, piece), f32),
        pltpu.VMEM((4, 16, quarter, piece), f32),
        pltpu.VMEM((16, 8, rank), f32),
        pltpu.VMEM((16, 8, rank), f32),
        pltpu.VMEM((8, 8, rank), f32),
        pltpu.VMEM((16, 8, rank), f32),
        DMA((8,)),
        *[DMA((3,))] * 4,
        *[DMA((4,))] * 2,
        *[DMA((4, 16))] * 2,
        *[DMA((16,))] * 2,
        *[DMA((8,))] * 2,
        *[DMA((16,))] * 2,
    ]
    if not first:
        scratch += [pltpu.VMEM((cols, rank), bf16), *[DMA((4, 16))] * 4]
    return pl.pallas_call(
        functools.partial(sweep_kernel, first),
        out_shape=(jax.ShapeDtypeStruct((rank, piece), f32), jax.ShapeDtypeStruct((rank, rank), f32)),
        in_specs=[SMEM, SMEM, ANY] + [VMEM] * len(panel),
        out_specs=(VMEM, VMEM),
        scratch_shapes=scratch,
        compiler_params=pltpu.CompilerParams(
            collective_id=number, has_side_effects=True, vmem_limit_bytes=VMEM_BYTES
        ),
        name=f"sweep_{number}",
    )(lengths, block_subject, scans, *panel)


def on_device(scans, test_matrix, lengths, block_subject):
    panel = (test_matrix,)
    for sweep in range(PASSES):
        panel = sweep_call(lengths, block_subject, scans, panel, sweep)
    return panel_call(*panel, PASSES).astype(f32)


def solution(mesh):
    placed = (P("subj", "vox"), P("vox", None), P(), P())
    return jax.shard_map(
        on_device, mesh=mesh, in_specs=placed, out_specs=P("vox", None), check_vma=False
    )
```

time: 501 us -> 166 us (0.33)
  waiting for transfers between devices: 318 us -> 0 us
  Pallas kernels: 0 us -> 161 us
  matrix products: 72.6 us -> 0 us
  other arithmetic: 53.3 us -> 4.32 us
  blocking collectives: 35.2 us -> 0 us
  between operations: 13.2 us -> 0.03 us
  local copies, waits for them, and re-layouts: 6.73 us -> 0 us
    psum x4 -> x0, waiting for transfers between devices: 318 us -> none  [the longest x2 240 us: on_device(): lax.psum(lax.dot_general(scans, scores, (((0,), (0,)), ((), ())), preferr...]
    pallas_call x0 -> x3, Pallas kernels: none -> 161 us  [the longest x2 136 us: sweep_call(): pl.pallas_call(functools.partial(sweep_kernel, first), out_shape=(jax.Sha...]
    dot_general x6 -> x0, matrix products: 55.8 us -> none  [the longest x2 22 us: on_device(): lax.dot_general(scans, scores, (((0,), (0,)), ((), ())), preferred_elemen...]
    another operation x10 -> x0, other arithmetic: 45.7 us -> none  [the longest x6 24.8 us: on_device(): factor = jnp.linalg.cholesky(gram_matrix)]
    psum x2 -> x0, blocking collectives: 35.2 us -> none  [on_device(): summed = lax.psum(partial_scores, 'vox')]
    another operation x2 -> x0, matrix products: 16.8 us -> none  [on_device(): jax.scipy.linalg.solve_triangular(factor, sketch.T, lower=True)]
    transpose x1 -> x0, local copies, waits for them, and re-layouts: 6.55 us -> none  [on_device(): jax.scipy.linalg.solve_triangular(factor, sketch.T, lower=True)]
  transfers between devices with their start and end apart: 4 -> 0, of which waited for: 4 -> 0; matrix products, arithmetic and copies ran while one was open for 0% -> 0% of each run, Pallas kernels for 0% -> 0%
where the time goes in v3:
time: 166 us
  Pallas kernels  161 us (97%)
  other arithmetic  4.32 us (3%)
    pallas_call x2, Pallas kernels, sweep_call(): pl.pallas_call(functools.partial(sweep_kernel, first), out_shape=(jax.Sha...  136 us
    pallas_call x1, Pallas kernels, panel_call(): pl.pallas_call(panel_kernel, out_shape=jax.ShapeDtypeStruct((32 * piece,...  25 us
    convert_element_type x1, other arithmetic, on_device(): return panel_call(*panel, PASSES).astype(f32)  4.32 us

profile of v3, /device:TPU:1, one launch (start us, length us, event | category | flops | bytes accessed | tf_op | source)
XLA Modules:
  0.0 165.6 jit_solution(1409748064692225185)
XLA Ops:
  0.0 60.8 %sweep_0.1 = (f32[128,384]{1,0:T(8,128)}, f32[128,128]{1,0:T(8,128)}) custom-call(s32[32]{0:T(128)} %refs_0_.3, s32[32]{0:T(128)} %refs_1_.3, bf16[640,12288]{1,0:T(8,128)(2,1)} %refs_2_.3, bf16[12288,128]{1,0:T(8,128)(2,1)} %refs_3_.1), custom_call_target="tpu_custom_call" | custom-call | tf_op jit(solution)/shard_map/sweep_0/pallas_call | solution.py:349
  60.8 75.5 %sweep_1.1 = (f32[128,384]{1,0:T(8,128)}, f32[128,128]{1,0:T(8,128)}) custom-call(s32[32]{0:T(128)} %refs_0_.3, s32[32]{0:T(128)} %refs_1_.3, bf16[640,12288]{1,0:T(8,128)(2,1)} %refs_2_.3, f32[128,384]{1,0:T(8,128)} %get-tuple-element.9.refs_3_, f32[128,128]{1,0:T(8,128)} %get-tuple-element.10.refs_4_), custom_call_target="tpu_custom_call" | custom-call | tf_op jit(solution)/shard_map/sweep_1/pallas_call | solution.py:349
  136.3 25.0 %panel_2.1 = bf16[12288,128]{1,0:T(8,128)(2,1)} custom-call(f32[128,384]{1,0:T(8,128)} %get-tuple-element.11.slice_t, f32[128,128]{1,0:T(8,128)} %get-tuple-element.12.gram), custom_call_target="tpu_custom_call" | custom-call | tf_op jit(solution)/shard_map/panel_2/pallas_call | solution.py:169
  161.3 4.3 %convert_element_type.3 = f32[12288,128]{1,0:T(8,128)} convert(bf16[12288,128]{1,0:T(8,128)(2,1)} %panel_2.1) | non-fusion elementwise | flops 1572864 | bytes 9437184 | tf_op jit(solution)/shard_map/convert_element_type | solution.py:366

commit v4 on v0

v4 whole, which is shorter than its diff:
```python
import jax
import jax.numpy as jnp
from jax import lax
from jax.experimental import pallas as pl
from jax.experimental.pallas import tpu as pltpu
from jax.sharding import PartitionSpec as P

V = 49152
PASSES = 2
MESH = pl.DeviceIdType.MESH
VMEM_BYTES = 46 * 2**20
ANY = pl.BlockSpec(memory_space=pl.ANY)
VMEM = pl.BlockSpec(memory_space=pltpu.VMEM)
SMEM = pl.BlockSpec(memory_space=pltpu.SMEM)
DMA = pltpu.SemaphoreType.DMA
f32, bf16 = jnp.float32, jnp.bfloat16
ORDERS = (("ya", "yb", "za", "zb"), ("yb", "ya", "zb", "za"), ("za", "zb", "ya", "yb"), ("zb", "za", "yb", "ya"))
WEIGHTS = (8, 4, 2, 1)


def flip_a(i):
    return i + 1 - 2 * lax.rem(i, 2)


def flip_b(i):
    return 3 - i


class Place:
    def __init__(self):
        here = lax.axis_index("subj")
        self.z, self.y, self.c = lax.div(here, 8), lax.rem(lax.div(here, 2), 4), lax.rem(here, 2)
        self.x = lax.axis_index("vox")

    def flipped(self, bits):
        z, y = self.z, self.y
        z = flip_a(z) if "za" in bits else z
        z = flip_b(z) if "zb" in bits else z
        y = flip_a(y) if "ya" in bits else y
        y = flip_b(y) if "yb" in bits else y
        return z, y

    def across(self, bit):
        z, y = self.flipped((bit,))
        return {"subj": z * 8 + y * 2 + self.c}

    def sibling(self):
        return {"subj": self.z * 8 + self.y * 2 + 1 - self.c}

    def in_plane(self, step):
        z, y = lax.rem(self.z + step // 4, 4), lax.rem(self.y + step % 4, 4)
        return z * 4 + y, {"subj": z * 8 + y * 2 + self.c}

    def along_x(self, step, other_core):
        x = lax.rem(self.x + step, 4)
        c = 1 - self.c if other_core else self.c
        return x * 2 + c, {"subj": self.z * 8 + self.y * 2 + c, "vox": x}


def flips_of(order, m):
    return tuple(bit for weight, bit in zip(WEIGHTS, order) if m & weight)


def pair_index(place, q, m):
    z, y = place.flipped(flips_of(ORDERS[q], m))
    return z * 4 + y


def greet(devices):
    barrier = pltpu.get_barrier_semaphore()
    for device in devices:
        pl.semaphore_signal(barrier, inc=1, device_id=device, device_id_type=MESH)
    return barrier, len(devices)


def send(src, dst, send_sem, recv_sem, device):
    copy = pltpu.make_async_remote_copy(
        src_ref=src, dst_ref=dst, send_sem=send_sem, recv_sem=recv_sem, device_id=device, device_id_type=MESH
    )
    copy.start()
    return copy


def landed(ref, sem):
    pltpu.make_async_copy(ref, ref, sem).wait()


def inverse_factor(gram):
    n, width = gram.shape[0], 8
    row, col = (lax.broadcasted_iota(jnp.int32, (n, n), d) for d in (0, 1))
    left, right = gram, (row == col).astype(jnp.float32)
    place = lax.broadcasted_iota(jnp.int32, (width, n), 0)
    done = []
    for k in range(0, n, width):
        columns = [jnp.broadcast_to(left[:, k + j : k + j + 1], left.shape) for j in range(width)]
        heads, tails = [c[:width] for c in columns], [c[width:] for c in columns]
        left_head, right_head = left[:width], right[:width]
        left, right = left[width:], right[width:]
        pivots = jnp.zeros((width, n), jnp.float32)
        for j in range(width):
            pivot = heads[j][j : j + 1]
            over = 1.0 / pivot
            pivots = jnp.where(place == j, jnp.broadcast_to(pivot, (width, n)), pivots)
            head = jnp.where(place > j, heads[j] * over, 0.0)
            left_row, right_row = left_head[j : j + 1], right_head[j : j + 1]
            if k + width < n:
                tail = tails[j] * over
                left, right = left - tail * left_row, right - tail * right_row
            for i in range(j + 1, width):
                factor = heads[j][i : i + 1]
                heads[i] = heads[i] - head * factor
                if k + width < n:
                    tails[i] = tails[i] - tail * factor
            left_head, right_head = left_head - head * left_row, right_head - head * right_row
        done.append(right_head * lax.rsqrt(pivots))
    return jnp.concatenate(done, 0)


def normalised(slice_t, gram):
    inverse = inverse_factor(gram / V)
    own = jnp.dot(inverse, slice_t[...], precision=lax.Precision.HIGHEST, preferred_element_type=f32)
    return own.T.astype(bf16)


def own_rows_in(place, own, panel):
    size = own.shape[0] // 4
    chunk = 4 * size

    def rows(core, q, m):
        start = (core * 16 + pair_index(place, q, m)) * chunk + q * size
        return panel.at[pl.ds(pl.multiple_of(start, 32), size)]

    for q in range(4):
        rows(place.c, q, 0)[...] = own[q * size : (q + 1) * size]
    return rows


def exchange_panel(place, rows, ss, rs, sc, rc):
    copies = []
    for m in (0, 1, 2, 4, 3, 5, 6, 7, 8, 9, 10, 12, 11, 13, 14, 15):
        for q in range(4):
            ref = rows(place.c, q, m)
            if m:
                landed(ref, rs.at[q, m])
            for weight, bit in ((1, 3), (2, 2), (4, 1), (8, 0)):
                if weight > m:
                    n = weight | m
                    copies.append(send(ref, ref, ss.at[q, n], rs.at[q, n], place.across(ORDERS[q][bit])))
            copies.append(send(ref, ref, sc.at[q, m], rc.at[q, m], place.sibling()))
    for q in range(4):
        for m in range(16):
            landed(rows(1 - place.c, q, m), rc.at[q, m])
    for copy in copies:
        copy.wait_send()


def whole_kernel(lengths, block_subject, scans, first_panel, out, *scratch):
    (
        held, panel, own_t, part, got, full, away, arrived, mine, inbox, g_part, g_in, g_side, g_full,
        load_sem, s1, r1, s2, r2, sc, rc, ss, rs, sg, rg, sh, rh, si, ri, sp, rp, sq, rq,
    ) = scratch
    place = Place()
    x = place.x
    rows = part.shape[1]
    rank, piece = own_t.shape
    quarter, width = rank // 4, 4 * piece
    owners = [lax.rem(x + step, 4) for step in (2, 1, 3, 0)]
    plane = [place.in_plane(step) for step in range(16)]
    beside = [(dx, dc, *place.along_x(dx, dc)) for dx in range(4) for dc in (0, 1) if dx or dc]
    greeted = greet([device for _, device in plane[1:]] + [device for *_, device in beside])

    def load(n):
        half = rows // 2
        at = pl.ds(pl.multiple_of(owners[n // 2] * rows + n % 2 * half, half), half)
        return pltpu.make_async_copy(scans.at[at], held.at[at], load_sem.at[n])

    ahead = 3
    for n in range(ahead):
        load(n).start()
    for sweep in range(PASSES):
        source = first_panel if sweep == 0 else panel
        tile = 3072
        copies = []
        for t in range(4):
            for n in (2 * t, 2 * t + 1):
                if sweep == 0 and n + ahead < 8:
                    load(n + ahead).start()
                if sweep == 0:
                    load(n).wait()

            def add(k, acc, t=t, source=source):
                at = pl.multiple_of(k * tile, tile)
                own_rows = pl.ds(pl.multiple_of(owners[t] * rows, rows), rows)
                return acc + jnp.dot(held[own_rows, pl.ds(at, tile)], source[pl.ds(at, tile), :], preferred_element_type=f32)

            part[t] = lax.fori_loop(0, source.shape[0] // tile, add, jnp.zeros(part.shape[1:], f32))
            if t == 0 and sweep == 0:
                pl.semaphore_wait(*greeted)
            if t < 3:
                copies.append(send(part.at[t], got.at[t], s1.at[t], r1.at[t], {"vox": owners[t]}))
        total = part[3]
        for t in range(3):
            copies[t].wait()
            total = total + got[t]
        length = lengths[block_subject[lax.axis_index("subj")]]
        time_ids = x * rows + lax.broadcasted_iota(jnp.int32, total.shape, 0)
        full[x] = jnp.where(time_ids < length, total, f32(0.0)).astype(bf16)
        copies = [send(full.at[x], full.at[x], s2.at[t], r2.at[t], {"vox": owners[t]}) for t in range(3)]
        for copy in copies:
            copy.wait()
        left = jnp.concatenate([full[i] for i in range(4)], 0).T

        z_flips = (("za", "zb"), ("za",), ("zb",), ())
        z_far = [place.flipped(flips)[0] for flips in z_flips]
        copies, core_copies = [], {}
        pair = [[pair_index(place, q, m) for m in range(16)] for q in range(4)]

        def pass_on(q, m, copies=copies):
            bit = ORDERS[q][4 - m.bit_length()]
            copies.append(send(mine.at[q, pair[q][m]], inbox.at[q, m], ss.at[q, m], rs.at[q, m], place.across(bit)))

        for away_side, k in ((1, 0), (1, 1), (0, 0), (1, 2), (0, 1), (1, 3), (0, 2), (0, 3)):
            core = 1 - place.c if away_side else place.c
            start = pl.multiple_of((core * 16 + z_far[k] * 4) * piece, width)
            block = jnp.dot(left, held[:, pl.ds(start, width)], preferred_element_type=f32)
            if not away_side:
                core_copies[k].wait()
            for y in range(4):
                for q in range(4):
                    value = block[q * quarter : (q + 1) * quarter, y * piece : (y + 1) * piece]
                    if away_side:
                        away[k, q, y] = value
                    else:
                        mine[q, z_far[k] * 4 + y] = value + arrived[k, q, y]
            if away_side:
                core_copies[k] = send(away.at[k], arrived.at[k], sc.at[k], rc.at[k], place.sibling())
                continue
            for m in range(15, 7, -1):
                for q in range(4):
                    if tuple(bit for bit in ("za", "zb") if bit in flips_of(ORDERS[q], m)) == z_flips[k]:
                        pass_on(q, m)

        for m in range(7, -1, -1):
            for q in range(4):
                value = mine[q, pair[q][m]]
                for weight in WEIGHTS:
                    if weight > m:
                        landed(inbox.at[q, weight | m], rs.at[q, weight | m])
                        value = value + inbox[q, weight | m]
                if m:
                    mine[q, pair[q][m]] = value
                    pass_on(q, m)
                else:
                    own_t[q * quarter : (q + 1) * quarter, :] = value

        own = own_t[...]
        gram = lax.dot_general(own, own, (((1,), (1,)), ((), ())), precision=lax.Precision.HIGHEST, preferred_element_type=f32)
        for p in range(16):
            g_part[p] = gram[8 * p : 8 * p + 8]
        here = plane[0][0]
        moved = [send(g_part.at[plane[r][0]], g_in.at[r], sg.at[r], rg.at[r], plane[r][1]) for r in range(1, 16)]
        for copy in copies:
            copy.wait_send()
        total = g_part[here]
        for r in range(1, 16):
            moved[r - 1].wait()
            total = total + g_in[r]
        me = x * 2 + place.c
        g_side[me] = total
        moved = [send(g_side.at[me], g_side.at[me], sh.at[n], rh.at[me], to[3]) for n, to in enumerate(beside)]
        for copy in moved:
            copy.wait_send()
        for to in beside:
            landed(g_side.at[to[2]], rh.at[to[2]])
        total = g_side[0]
        for n in range(1, 8):
            total = total + g_side[n]
        g_full[here] = total
        moved = [send(g_full.at[here], g_full.at[here], si.at[r], ri.at[r], plane[r][1]) for r in range(1, 16)]
        for copy in moved:
            copy.wait()

        target = out if sweep == PASSES - 1 else panel
        gram = jnp.concatenate([g_full[p] for p in range(16)], 0)
        slices = own_rows_in(place, normalised(own_t, gram), target)
        exchange_panel(place, slices, sp, rp, sq, rq)


def whole_call(lengths, block_subject, scans, panel):
    time_rows, cols = scans.shape
    rank = panel.shape[1]
    piece, quarter, rows = cols // 32, rank // 4, time_rows // 4
    return pl.pallas_call(
        whole_kernel,
        out_shape=jax.ShapeDtypeStruct((cols, rank), bf16),
        in_specs=[SMEM, SMEM, ANY, VMEM],
        out_specs=VMEM,
        scratch_shapes=[
            pltpu.VMEM((time_rows, cols), bf16),
            pltpu.VMEM((cols, rank), bf16),
            pltpu.VMEM((rank, piece), f32),
            pltpu.VMEM((4, rows, rank), f32),
            pltpu.VMEM((3, rows, rank), f32),
            pltpu.VMEM((4, rows, rank), bf16),
            pltpu.VMEM((4, 4, 4, quarter, piece), f32),
            pltpu.VMEM((4, 4, 4, quarter, piece), f32),
            pltpu.VMEM((4, 16, quarter, piece), f32),
            pltpu.VMEM((4, 16, quarter, piece), f32),
            pltpu.VMEM((16, 8, rank), f32),
            pltpu.VMEM((16, 8, rank), f32),
            pltpu.VMEM((8, 8, rank), f32),
            pltpu.VMEM((16, 8, rank), f32),
            DMA((8,)),
            *[DMA((3,))] * 4,
            *[DMA((4,))] * 2,
            *[DMA((4, 16))] * 2,
            *[DMA((16,))] * 2,
            *[DMA((8,))] * 2,
            *[DMA((16,))] * 2,
            *[DMA((4, 16))] * 4,
        ],
        compiler_params=pltpu.CompilerParams(
            collective_id=0, has_side_effects=True, vmem_limit_bytes=VMEM_BYTES
        ),
        name="range_finder",
    )(lengths, block_subject, scans, panel)


def on_device(scans, test_matrix, lengths, block_subject):
    return whole_call(lengths, block_subject, scans, test_matrix).astype(f32)


def solution(mesh):
    placed = (P("subj", "vox"), P("vox", None), P(), P())
    return jax.shard_map(
        on_device, mesh=mesh, in_specs=placed, out_specs=P("vox", None), check_vma=False
    )
```

time: 501 us -> 157 us (0.31)
  waiting for transfers between devices: 318 us -> 0 us
  Pallas kernels: 0 us -> 151 us
  matrix products: 72.6 us -> 0 us
  other arithmetic: 53.3 us -> 2.93 us
  blocking collectives: 35.2 us -> 0 us
  between operations: 13.2 us -> 0.01 us
    psum x4 -> x0, waiting for transfers between devices: 318 us -> none  [the longest x2 240 us: on_device(): lax.psum(lax.dot_general(scans, scores, (((0,), (0,)), ((), ())), preferr...]
    pallas_call x0 -> x1, Pallas kernels: none -> 151 us  [whole_call(): pl.pallas_call(whole_kernel, out_shape=jax.ShapeDtypeStruct((cols, rank),...]
    dot_general x6 -> x0, matrix products: 55.8 us -> none  [the longest x2 22 us: on_device(): lax.dot_general(scans, scores, (((0,), (0,)), ((), ())), preferred_elemen...]
    another operation x10 -> x0, other arithmetic: 45.7 us -> none  [the longest x6 24.8 us: on_device(): factor = jnp.linalg.cholesky(gram_matrix)]
    psum x2 -> x0, blocking collectives: 35.2 us -> none  [on_device(): summed = lax.psum(partial_scores, 'vox')]
    another operation x2 -> x0, matrix products: 16.8 us -> none  [on_device(): jax.scipy.linalg.solve_triangular(factor, sketch.T, lower=True)]
    transpose x1 -> x0, local copies, waits for them, and re-layouts: 6.55 us -> none  [on_device(): jax.scipy.linalg.solve_triangular(factor, sketch.T, lower=True)]
  transfers between devices with their start and end apart: 4 -> 0, of which waited for: 4 -> 0; matrix products, arithmetic and copies ran while one was open for 0% -> 0% of each run, Pallas kernels for 0% -> 0%
where the time goes in v4:
time: 157 us
  Pallas kernels  151 us (96%)
  local copies, waits for them, and re-layouts  3.2 us (2%)
  other arithmetic  2.93 us (2%)
    pallas_call x1, Pallas kernels, whole_call(): pl.pallas_call(whole_kernel, out_shape=jax.ShapeDtypeStruct((cols, rank),...  151 us
    unnamed x6, local copies, waits for them, and re-layouts  3.2 us

profile of v4, /device:TPU:1, one launch (start us, length us, event | category | flops | bytes accessed | tf_op | source)
XLA Modules:
  0.0 156.9 jit_solution(2962685433259610006)
XLA Ops:
  0.0 0.0 copy-start
  0.0 1.9 %copy-done = bf16[12288,128]{1,0:T(8,128)(2,1)S(1)} copy-done((bf16[12288,128]{1,0:T(8,128)(2,1)S(1)}, bf16[12288,128]{1,0:T(8,128)(2,1)}, u32[]{:S(2)}) %copy-start) | copy-done | bytes 3145752
  1.9 0.0 copy-start.1
  1.9 0.7 copy-done.1
  2.5 0.0 copy-start.2
  2.5 0.7 copy-done.2
  3.2 150.7 %range_finder.1 = bf16[12288,128]{1,0:T(8,128)(2,1)S(1)} custom-call(s32[32]{0:T(128)S(1)} %copy-done.1, s32[32]{0:T(128)S(1)} %copy-done.2, bf16[640,12288]{1,0:T(8,128)(2,1)} %scans.1, bf16[12288,128]{1,0:T(8,128)(2,1)S(1)} %copy-done), custom_call_target="tpu_custom_call" | custom-call | tf_op jit(solution)/shard_map/range_finder/pallas_call | solution.py:293
  154.0 2.9 %convert_element_type.3 = f32[12288,128]{1,0:T(8,128)} convert(bf16[12288,128]{1,0:T(8,128)(2,1)S(1)} %range_finder.1) | non-fusion elementwise | flops 1572864 | bytes 9437184 | tf_op jit(solution)/shard_map/convert_element_type | solution.py:330
Async XLA Ops:
  0.0 1.9 %copy-start = (bf16[12288,128]{1,0:T(8,128)(2,1)S(1)}, bf16[12288,128]{1,0:T(8,128)(2,1)}, u32[]{:S(2)}) copy-start(bf16[12288,128]{1,0:T(8,128)(2,1)} %first_panel.1) | copy-start | bytes 9437188
  1.9 0.7 copy-start.1
  2.5 0.7 copy-start.2

commit v5 on v4

--- a/solution.py
+++ b/solution.py
@@ -9,9 +9,8 @@
 PASSES = 2
 MESH = pl.DeviceIdType.MESH
 VMEM_BYTES = 46 * 2**20
-ANY = pl.BlockSpec(memory_space=pl.ANY)
 VMEM = pl.BlockSpec(memory_space=pltpu.VMEM)
-SMEM = pl.BlockSpec(memory_space=pltpu.SMEM)
+HBM = pl.BlockSpec(memory_space=pltpu.HBM)
 DMA = pltpu.SemaphoreType.DMA
 f32, bf16 = jnp.float32, jnp.bfloat16
 ORDERS = (("ya", "yb", "za", "zb"), ("yb", "ya", "zb", "za"), ("za", "zb", "ya", "yb"), ("zb", "za", "yb", "ya"))
@@ -154,9 +153,9 @@
         copy.wait_send()
 
 
-def whole_kernel(lengths, block_subject, scans, first_panel, out, *scratch):
+def whole_kernel(lengths_in, block_subject_in, scans, panel_in, out, *scratch):
     (
-        held, panel, own_t, part, got, full, away, arrived, mine, inbox, g_part, g_in, g_side, g_full,
+        lengths, block_subject, small_sem, first_panel, held, panel, own_t, part, got, full, away, arrived, mine, inbox, g_part, g_in, g_side, g_full,
         load_sem, s1, r1, s2, r2, sc, rc, ss, rs, sg, rg, sh, rh, si, ri, sp, rp, sq, rq,
     ) = scratch
     place = Place()
@@ -174,12 +173,20 @@
         at = pl.ds(pl.multiple_of(owners[n // 2] * rows + n % 2 * half, half), half)
         return pltpu.make_async_copy(scans.at[at], held.at[at], load_sem.at[n])
 
+    small = [
+        pltpu.make_async_copy(panel_in, first_panel, small_sem.at[0]),
+        pltpu.make_async_copy(lengths_in, lengths, small_sem.at[1]),
+        pltpu.make_async_copy(block_subject_in, block_subject, small_sem.at[2]),
+    ]
+    for copy in small:
+        copy.start()
     ahead = 3
     for n in range(ahead):
         load(n).start()
+    for copy in small:
+        copy.wait()
     for sweep in range(PASSES):
         source = first_panel if sweep == 0 else panel
-        tile = 3072
         copies = []
         for t in range(4):
             for n in (2 * t, 2 * t + 1):
@@ -188,12 +195,14 @@
                 if sweep == 0:
                     load(n).wait()
 
-            def add(k, acc, t=t, source=source):
-                at = pl.multiple_of(k * tile, tile)
-                own_rows = pl.ds(pl.multiple_of(owners[t] * rows, rows), rows)
-                return acc + jnp.dot(held[own_rows, pl.ds(at, tile)], source[pl.ds(at, tile), :], preferred_element_type=f32)
-
-            part[t] = lax.fori_loop(0, source.shape[0] // tile, add, jnp.zeros(part.shape[1:], f32))
+            own_rows = pl.ds(pl.multiple_of(owners[t] * rows, rows), rows)
+            tile = source.shape[0] // 2
+
+            def add(k, acc, own_rows=own_rows, source=source, tile=tile):
+                at = pl.ds(pl.multiple_of(k * tile, tile), tile)
+                return acc + jnp.dot(held[own_rows, at], source[at, :], preferred_element_type=f32)
+
+            part[t] = lax.fori_loop(0, 2, add, jnp.zeros(part.shape[1:], f32))
             if t == 0 and sweep == 0:
                 pl.semaphore_wait(*greeted)
             if t < 3:
@@ -235,12 +244,12 @@
             if away_side:
                 core_copies[k] = send(away.at[k], arrived.at[k], sc.at[k], rc.at[k], place.sibling())
                 continue
-            for m in range(15, 7, -1):
+            for m in range(15, 11, -1):
                 for q in range(4):
                     if tuple(bit for bit in ("za", "zb") if bit in flips_of(ORDERS[q], m)) == z_flips[k]:
                         pass_on(q, m)
 
-        for m in range(7, -1, -1):
+        for m in (7, 6, 5, 3, 4, 2, 1, 0):
             for q in range(4):
                 value = mine[q, pair[q][m]]
                 for weight in WEIGHTS:
@@ -250,6 +259,8 @@
                 if m:
                     mine[q, pair[q][m]] = value
                     pass_on(q, m)
+                    if m > 3:
+                        pass_on(q, m + 4)
                 else:
                     own_t[q * quarter : (q + 1) * quarter, :] = value
 
@@ -293,9 +304,13 @@
     return pl.pallas_call(
         whole_kernel,
         out_shape=jax.ShapeDtypeStruct((cols, rank), bf16),
-        in_specs=[SMEM, SMEM, ANY, VMEM],
+        in_specs=[HBM, HBM, HBM, HBM],
         out_specs=VMEM,
         scratch_shapes=[
+            pltpu.SMEM(lengths.shape, jnp.int32),
+            pltpu.SMEM(block_subject.shape, jnp.int32),
+            DMA((3,)),
+            pltpu.VMEM((cols, rank), bf16),
             pltpu.VMEM((time_rows, cols), bf16),
             pltpu.VMEM((cols, rank), bf16),
             pltpu.VMEM((rank, piece), f32),
@@ -327,6 +342,9 @@
 
 
 def on_device(scans, test_matrix, lengths, block_subject):
+    lengths, block_subject, test_matrix = (
+        pltpu.with_memory_space_constraint(a, pltpu.HBM) for a in (lengths, block_subject, test_matrix)
+    )
     return whole_call(lengths, block_subject, scans, test_matrix).astype(f32)
 
 

time: 157 us -> 150 us (0.955)
  Pallas kernels: 151 us -> 147 us
  local copies, waits for them, and re-layouts: 3.2 us -> 0 us
    pallas_call x1, Pallas kernels: 151 us -> 147 us  [whole_call(): pl.pallas_call(whole_kernel, out_shape=jax.ShapeDtypeStruct((cols, rank),...]
    unnamed x6 -> x0, local copies, waits for them, and re-layouts: 3.2 us -> none
where the time goes in v5:
time: 150 us
  Pallas kernels  147 us (98%)
  other arithmetic  2.93 us (2%)
    pallas_call x1, Pallas kernels, whole_call(): pl.pallas_call(whole_kernel, out_shape=jax.ShapeDtypeStruct((cols, rank),...  147 us

profile of v5, /device:TPU:1, one launch (start us, length us, event | category | flops | bytes accessed | tf_op | source)
XLA Modules:
  0.0 149.6 jit_solution(10970729891065652470)
XLA Ops:
  0.0 146.7 %range_finder.1 = bf16[12288,128]{1,0:T(8,128)(2,1)S(1)} custom-call(s32[32]{0:T(128)} %lengths_in.1, s32[32]{0:T(128)} %block_subject_in.1, bf16[640,12288]{1,0:T(8,128)(2,1)} %scans.1, bf16[12288,128]{1,0:T(8,128)(2,1)} %panel_in.1), custom_call_target="tpu_custom_call" | custom-call | tf_op jit(solution)/shard_map/range_finder/pallas_call | solution.py:304
  146.7 2.9 %convert_element_type.3 = f32[12288,128]{1,0:T(8,128)} convert(bf16[12288,128]{1,0:T(8,128)(2,1)S(1)} %range_finder.1) | non-fusion elementwise | flops 1572864 | bytes 9437184 | tf_op jit(solution)/shard_map/convert_element_type | solution.py:348

commit v6 on v5

--- a/solution.py
+++ b/solution.py
@@ -31,20 +31,25 @@
         self.z, self.y, self.c = lax.div(here, 8), lax.rem(lax.div(here, 2), 4), lax.rem(here, 2)
         self.x = lax.axis_index("vox")
 
-    def flipped(self, bits):
-        z, y = self.z, self.y
-        z = flip_a(z) if "za" in bits else z
-        z = flip_b(z) if "zb" in bits else z
-        y = flip_a(y) if "ya" in bits else y
-        y = flip_b(y) if "yb" in bits else y
-        return z, y
+        self.zs = {(): self.z, ("za",): flip_a(self.z), ("zb",): flip_b(self.z)}
+        self.zs["za", "zb"] = flip_b(self.zs[("za",)])
+        self.ys = {(): self.y, ("ya",): flip_a(self.y), ("yb",): flip_b(self.y)}
+        self.ys["ya", "yb"] = flip_b(self.ys[("ya",)])
+        self.to = {
+            bit: {"subj": (self.zs if bit[0] == "z" else self.ys)[(bit,)] * (8 if bit[0] == "z" else 2) + rest + self.c}
+            for bit in ORDERS[0]
+            for rest in [self.y * 2 if bit[0] == "z" else self.z * 8]
+        }
+        self.pairs = {
+            zf + yf: z * 4 + y for zf, z in self.zs.items() for yf, y in self.ys.items()
+        }
+        self.beside_core = {"subj": here + 1 - 2 * self.c}
 
     def across(self, bit):
-        z, y = self.flipped((bit,))
-        return {"subj": z * 8 + y * 2 + self.c}
+        return self.to[bit]
 
     def sibling(self):
-        return {"subj": self.z * 8 + self.y * 2 + 1 - self.c}
+        return self.beside_core
 
     def in_plane(self, step):
         z, y = lax.rem(self.z + step // 4, 4), lax.rem(self.y + step % 4, 4)
@@ -57,12 +62,12 @@
 
 
 def flips_of(order, m):
-    return tuple(bit for weight, bit in zip(WEIGHTS, order) if m & weight)
+    flips = [bit for weight, bit in zip(WEIGHTS, order) if m & weight]
+    return tuple(bit for bit in ("za", "zb", "ya", "yb") if bit in flips)
 
 
 def pair_index(place, q, m):
-    z, y = place.flipped(flips_of(ORDERS[q], m))
-    return z * 4 + y
+    return place.pairs[flips_of(ORDERS[q], m)]
 
 
 def greet(devices):
@@ -121,41 +126,45 @@
     return own.T.astype(bf16)
 
 
-def own_rows_in(place, own, panel):
-    size = own.shape[0] // 4
-    chunk = 4 * size
-
-    def rows(core, q, m):
-        start = (core * 16 + pair_index(place, q, m)) * chunk + q * size
-        return panel.at[pl.ds(pl.multiple_of(start, 32), size)]
-
+def exchange_panel(place, own, panel, ss, rs, sc, rc):
+    chunk = own.shape[0]
+    size = chunk // 4
+
+    def rows(core, pair, q=None):
+        start = (core * 16 + pair) * chunk
+        if q is None:
+            return panel.at[pl.ds(pl.multiple_of(start, 32), chunk)]
+        return panel.at[pl.ds(pl.multiple_of(start + q * size, 32), size)]
+
+    def pass_on(q, m, weight):
+        ref = rows(place.c, pair_index(place, q, m), q)
+        device = {"subj": place.pairs[flips_of(ORDERS[q], weight)] * 2 + place.c}
+        send(ref, ref, ss.at[q], rs.at[q, weight | m], device)
+
+    rows(place.c, place.pairs[()])[...] = own
+    for weight in (1, 2, 3, 4, 8):
+        for q in range(4):
+            pass_on(q, 0, weight)
+    for m in range(16):
+        for q in range(4):
+            if m:
+                landed(rows(place.c, pair_index(place, q, m), q), rs.at[q, m])
+                for weight in (4, 8):
+                    if weight > m:
+                        pass_on(q, m, weight)
+        for flips, pair in place.pairs.items():
+            if m == max(sum(w for w, bit in zip(WEIGHTS, order) if bit in flips) for order in ORDERS):
+                send(rows(place.c, pair), rows(place.c, pair), sc.at[0], rc.at[0], place.sibling())
+    half = panel.at[pl.ds(0, 16 * chunk)]
     for q in range(4):
-        rows(place.c, q, 0)[...] = own[q * size : (q + 1) * size]
-    return rows
-
-
-def exchange_panel(place, rows, ss, rs, sc, rc):
-    copies = []
-    for m in (0, 1, 2, 4, 3, 5, 6, 7, 8, 9, 10, 12, 11, 13, 14, 15):
-        for q in range(4):
-            ref = rows(place.c, q, m)
-            if m:
-                landed(ref, rs.at[q, m])
-            for weight, bit in ((1, 3), (2, 2), (4, 1), (8, 0)):
-                if weight > m:
-                    n = weight | m
-                    copies.append(send(ref, ref, ss.at[q, n], rs.at[q, n], place.across(ORDERS[q][bit])))
-            copies.append(send(ref, ref, sc.at[q, m], rc.at[q, m], place.sibling()))
-    for q in range(4):
-        for m in range(16):
-            landed(rows(1 - place.c, q, m), rc.at[q, m])
-    for copy in copies:
-        copy.wait_send()
+        landed(panel.at[pl.ds(0, 15 * size)], ss.at[q])
+    landed(half, sc.at[0])
+    landed(half, rc.at[0])
 
 
 def whole_kernel(lengths_in, block_subject_in, scans, panel_in, out, *scratch):
     (
-        lengths, block_subject, small_sem, first_panel, held, panel, own_t, part, got, full, away, arrived, mine, inbox, g_part, g_in, g_side, g_full,
+        lengths, block_subject, small_sem, first_panel, held, panel, own_t, part, got, full, away, arrived, mine, inbox, g_part, g_in, g_plane, g_full,
         load_sem, s1, r1, s2, r2, sc, rc, ss, rs, sg, rg, sh, rh, si, ri, sp, rp, sq, rq,
     ) = scratch
     place = Place()
@@ -220,13 +229,13 @@
         left = jnp.concatenate([full[i] for i in range(4)], 0).T
 
         z_flips = (("za", "zb"), ("za",), ("zb",), ())
-        z_far = [place.flipped(flips)[0] for flips in z_flips]
-        copies, core_copies = [], {}
+        z_far = [place.zs[flips] for flips in z_flips]
+        core_copies = {}
         pair = [[pair_index(place, q, m) for m in range(16)] for q in range(4)]
 
-        def pass_on(q, m, copies=copies):
+        def pass_on(q, m):
             bit = ORDERS[q][4 - m.bit_length()]
-            copies.append(send(mine.at[q, pair[q][m]], inbox.at[q, m], ss.at[q, m], rs.at[q, m], place.across(bit)))
+            send(mine.at[q, pair[q][m]], inbox.at[q, m], ss.at[q], rs.at[q, m], place.across(bit))
 
         for away_side, k in ((1, 0), (1, 1), (0, 0), (1, 2), (0, 1), (1, 3), (0, 2), (0, 3)):
             core = 1 - place.c if away_side else place.c
@@ -266,35 +275,32 @@
 
         own = own_t[...]
         gram = lax.dot_general(own, own, (((1,), (1,)), ((), ())), precision=lax.Precision.HIGHEST, preferred_element_type=f32)
-        for p in range(16):
-            g_part[p] = gram[8 * p : 8 * p + 8]
-        here = plane[0][0]
-        moved = [send(g_part.at[plane[r][0]], g_in.at[r], sg.at[r], rg.at[r], plane[r][1]) for r in range(1, 16)]
-        for copy in copies:
-            copy.wait_send()
-        total = g_part[here]
-        for r in range(1, 16):
-            moved[r - 1].wait()
-            total = total + g_in[r]
-        me = x * 2 + place.c
-        g_side[me] = total
-        moved = [send(g_side.at[me], g_side.at[me], sh.at[n], rh.at[me], to[3]) for n, to in enumerate(beside)]
-        for copy in moved:
-            copy.wait_send()
-        for to in beside:
-            landed(g_side.at[to[2]], rh.at[to[2]])
-        total = g_side[0]
-        for n in range(1, 8):
-            total = total + g_side[n]
-        g_full[here] = total
-        moved = [send(g_full.at[here], g_full.at[here], si.at[r], ri.at[r], plane[r][1]) for r in range(1, 16)]
+        block = rank // 8
+        for p in range(8):
+            g_part[p] = gram[block * p : block * (p + 1)]
+        me, here = x * 2 + place.c, plane[0][0]
+        moved = [send(g_part.at[to[2]], g_in.at[n], sg.at[n], rg.at[n], to[3]) for n, to in enumerate(beside)]
+        for q in range(4):
+            landed(mine.at[q, pl.ds(0, 15)], ss.at[q])
+        total = g_part[me]
+        for n, copy in enumerate(moved):
+            copy.wait()
+            total = total + g_in[n]
+        g_plane[here] = total
+        moved = [send(g_plane.at[here], g_plane.at[here], sh.at[r], rh.at[r], plane[r][1]) for r in range(1, 16)]
         for copy in moved:
             copy.wait()
+        total = g_plane[0]
+        for p in range(1, 16):
+            total = total + g_plane[p]
+        g_full[me] = total
+        moved = [send(g_full.at[me], g_full.at[me], si.at[n], ri.at[n], to[3]) for n, to in enumerate(beside)]
+        for copy in moved:
+            copy.wait()
 
         target = out if sweep == PASSES - 1 else panel
-        gram = jnp.concatenate([g_full[p] for p in range(16)], 0)
-        slices = own_rows_in(place, normalised(own_t, gram), target)
-        exchange_panel(place, slices, sp, rp, sq, rq)
+        gram = jnp.concatenate([g_full[p] for p in range(8)], 0)
+        exchange_panel(place, normalised(own_t, gram), target, sp, rp, sq, rq)
 
 
 def whole_call(lengths, block_subject, scans, panel):
@@ -321,18 +327,21 @@
             pltpu.VMEM((4, 4, 4, quarter, piece), f32),
             pltpu.VMEM((4, 16, quarter, piece), f32),
             pltpu.VMEM((4, 16, quarter, piece), f32),
-            pltpu.VMEM((16, 8, rank), f32),
-            pltpu.VMEM((16, 8, rank), f32),
-            pltpu.VMEM((8, 8, rank), f32),
-            pltpu.VMEM((16, 8, rank), f32),
+            pltpu.VMEM((8, rank // 8, rank), f32),
+            pltpu.VMEM((7, rank // 8, rank), f32),
+            pltpu.VMEM((16, rank // 8, rank), f32),
+            pltpu.VMEM((8, rank // 8, rank), f32),
             DMA((8,)),
             *[DMA((3,))] * 4,
             *[DMA((4,))] * 2,
-            *[DMA((4, 16))] * 2,
+            DMA((4,)),
+            DMA((4, 16)),
+            *[DMA((7,))] * 2,
             *[DMA((16,))] * 2,
-            *[DMA((8,))] * 2,
-            *[DMA((16,))] * 2,
-            *[DMA((4, 16))] * 4,
+            *[DMA((7,))] * 2,
+            DMA((4,)),
+            DMA((4, 16)),
+            *[DMA((1,))] * 2,
         ],
         compiler_params=pltpu.CompilerParams(
             collective_id=0, has_side_effects=True, vmem_limit_bytes=VMEM_BYTES

time: 150 us -> 144 us (0.960)
  Pallas kernels: 147 us -> 141 us
    pallas_call x1, Pallas kernels: 147 us -> 141 us  [whole_call(): pl.pallas_call(whole_kernel, out_shape=jax.ShapeDtypeStruct((cols, rank),...]
where the time goes in v6:
time: 144 us
  Pallas kernels  141 us (98%)
  other arithmetic  2.93 us (2%)
    pallas_call x1, Pallas kernels, whole_call(): pl.pallas_call(whole_kernel, out_shape=jax.ShapeDtypeStruct((cols, rank),...  141 us
    convert_element_type x1, other arithmetic, on_device(): return whole_call(lengths, block_subject, scans, test_matrix).astype(f32)  2.93 us

profile of v6, /device:TPU:1, one launch (start us, length us, event | category | flops | bytes accessed | tf_op | source)
XLA Modules:
  0.0 143.6 jit_solution(8475175343755269108)
XLA Ops:
  0.0 140.7 %range_finder.1 = bf16[12288,128]{1,0:T(8,128)(2,1)S(1)} custom-call(s32[32]{0:T(128)} %lengths_in.1, s32[32]{0:T(128)} %block_subject_in.1, bf16[640,12288]{1,0:T(8,128)(2,1)} %scans.1, bf16[12288,128]{1,0:T(8,128)(2,1)} %panel_in.1), custom_call_target="tpu_custom_call" | custom-call | tf_op jit(solution)/shard_map/range_finder/pallas_call | solution.py:310
  140.7 2.9 %convert_element_type.3 = f32[12288,128]{1,0:T(8,128)} convert(bf16[12288,128]{1,0:T(8,128)(2,1)S(1)} %range_finder.1) | non-fusion elementwise | flops 1572864 | bytes 9437184 | tf_op jit(solution)/shard_map/convert_element_type | solution.py:357

commit v7 on v6

--- a/solution.py
+++ b/solution.py
@@ -205,13 +205,7 @@
                     load(n).wait()
 
             own_rows = pl.ds(pl.multiple_of(owners[t] * rows, rows), rows)
-            tile = source.shape[0] // 2
-
-            def add(k, acc, own_rows=own_rows, source=source, tile=tile):
-                at = pl.ds(pl.multiple_of(k * tile, tile), tile)
-                return acc + jnp.dot(held[own_rows, at], source[at, :], preferred_element_type=f32)
-
-            part[t] = lax.fori_loop(0, 2, add, jnp.zeros(part.shape[1:], f32))
+            part[t] = jnp.dot(held[own_rows, :], source[...], preferred_element_type=f32)
             if t == 0 and sweep == 0:
                 pl.semaphore_wait(*greeted)
             if t < 3:

time: 144 us -> 143 us (level)
  no operation moved by 1% of the time
where the time goes in v7:
time: 143 us
  Pallas kernels  140 us (98%)
  other arithmetic  2.93 us (2%)
    pallas_call x1, Pallas kernels, whole_call(): pl.pallas_call(whole_kernel, out_shape=jax.ShapeDtypeStruct((cols, rank),...  140 us
    convert_element_type x1, other arithmetic, on_device(): return whole_call(lengths, block_subject, scans, test_matrix).astype(f32)  2.93 us

profile of v7, /device:TPU:1, one launch (start us, length us, event | category | flops | bytes accessed | tf_op | source)
XLA Modules:
  0.0 143.1 jit_solution(11266972120489070315)
XLA Ops:
  0.0 140.2 %range_finder.1 = bf16[12288,128]{1,0:T(8,128)(2,1)S(1)} custom-call(s32[32]{0:T(128)} %lengths_in.1, s32[32]{0:T(128)} %block_subject_in.1, bf16[640,12288]{1,0:T(8,128)(2,1)} %scans.1, bf16[12288,128]{1,0:T(8,128)(2,1)} %panel_in.1), custom_call_target="tpu_custom_call" | custom-call | tf_op jit(solution)/shard_map/range_finder/pallas_call | solution.py:304
  140.2 2.9 %convert_element_type.3 = f32[12288,128]{1,0:T(8,128)} convert(bf16[12288,128]{1,0:T(8,128)(2,1)S(1)} %range_finder.1) | non-fusion elementwise | flops 1572864 | bytes 9437184 | tf_op jit(solution)/shard_map/convert_element_type | solution.py:351
